TPU v7x, 32 devices: a whole 2x2x4 slice. The times are simulated.
32 devices in a mesh: grp: 2 (over y), row: 4 (over z), col: 2 (over x), sub: 2 (over core).
Axes of the slice: x: 2, y: 2, z: 4, core: 2. Of those that a mesh axis runs over, the one named last changes fastest.
Arguments:
- pair: bfloat16 [768, 384, 128], P(('grp', 'row'), ('col', 'sub')), parts along dimension 0, may hold values from -6 to 6
- chain_ids: int32 [768], P('grp'), parts along dimension 0, may hold values from 0 to 3, never falling along the last dimension, each value on 1 to 192 neighbouring positions
- residue_mask: int32 [768], P('grp'), parts along dimension 0, may hold values from 0 to 1, as said below
- chain_vec: float32 [128], replicated, may hold values from -4 to 4
- tri_in: bfloat16 [128, 512], replicated, may hold values from -0.5 to 0.5
- tri_gate: bfloat16 [128, 128], replicated, may hold values from -0.5 to 0.5
- tri_out: bfloat16 [128, 128], replicated, may hold values from -0.5 to 0.5
- att_query: bfloat16 [128, 256], replicated, may hold values from -0.5 to 0.5
- att_kv: bfloat16 [128, 256], replicated, may hold values from -0.5 to 0.5
- att_bias: bfloat16 [128, 4], replicated, may hold values from -0.5 to 0.5
- att_out: bfloat16 [128, 128], replicated, may hold values from -0.5 to 0.5
Outputs:
- updated: bfloat16 [768, 384, 128], P(('grp', 'row'), ('col', 'sub')), parts along dimension 0
There are 2 independent parts, one for each index of `grp`. A program takes and returns all parts, laid end to end along the dimension named above; an argument that names none is the same for every part. Nothing has to cross between parts.
Inputs may be any that keep to these rules, and one draw needn't show every extreme that they name: `chain_ids`: chains are runs of consecutive residues. `residue_mask`: 1 on residues 0 to L - 1 and 0 after them, with L between 192 and 384.
All inputs are finite; a program needn't handle non-finite values.
Results may differ from a plain program's by a relative error of at most 0.009.
Values may be sent and summed in bfloat16 or wider, within the bound.
A program may use at most 128 MiB of HBM per device.

v0:
```python
import jax
import jax.numpy as jnp
from jax import lax
from jax.sharding import PartitionSpec as P

HEADS = 4
HEAD_DIM = 32


EPSILON = 1e-05


def layer_norm(values):
    average = jnp.mean(values, axis=-1, keepdims=True)
    centred = values - average
    spread = jnp.mean(centred * centred, axis=-1, keepdims=True)
    return centred * lax.rsqrt(spread + EPSILON)


def on_device(
    pair,
    chain_ids,
    residue_mask,
    chain_vec,
    tri_in,
    tri_gate,
    tri_out,
    att_query,
    att_kv,
    att_bias,
    att_out,
):
    rows, cols, channels = pair.shape
    heads_width = HEADS * HEAD_DIM
    row_start = lax.axis_index("row") * rows
    col_block = lax.axis_index(("col", "sub"))
    col_start = col_block * cols
    living = residue_mask.astype(jnp.float32)
    row_live = lax.dynamic_slice_in_dim(living, row_start, rows)
    col_live = lax.dynamic_slice_in_dim(living, col_start, cols)
    row_chain = lax.dynamic_slice_in_dim(chain_ids, row_start, rows)
    col_chain = lax.dynamic_slice_in_dim(chain_ids, col_start, cols)
    same_chain = (row_chain[:, None] == col_chain[None, :]).astype(jnp.float32)
    pair_mask = row_live[:, None] * col_live[None, :]
    start_pair = pair.astype(jnp.float32) + same_chain[:, :, None] * chain_vec
    normed = layer_norm(start_pair).astype(jnp.bfloat16)
    flat_rows = normed.reshape(rows * cols, channels)
    projected = jnp.dot(flat_rows, tri_in, preferred_element_type=jnp.float32).reshape(
        rows, cols, 4 * channels
    )
    left_side = (
        jax.nn.sigmoid(projected[..., channels : 2 * channels])
        * projected[..., :channels]
        * pair_mask[..., None]
    )
    right_side = (
        jax.nn.sigmoid(projected[..., 3 * channels :])
        * projected[..., 2 * channels : 3 * channels]
        * pair_mask[..., None]
    )
    stacked = jnp.transpose(jnp.stack([left_side, right_side]).astype(jnp.bfloat16), (0, 3, 1, 2))
    regrouped = lax.all_to_all(
        lax.all_to_all(stacked, "row", split_axis=1, concat_axis=2, tiled=True),
        ("col", "sub"),
        split_axis=2,
        concat_axis=3,
        tiled=True,
    )
    left_part = regrouped[0]
    right_part = regrouped[1]
    product = jnp.einsum(
        "cjk,cik->cji",
        right_part,
        lax.all_gather(left_part, ("col", "sub"), axis=1, tiled=True),
        preferred_element_type=jnp.float32,
    ).astype(jnp.bfloat16)
    returned = lax.all_to_all(product, "row", split_axis=2, concat_axis=0, tiled=True)
    product_pairs = jnp.transpose(returned, (2, 1, 0)).astype(jnp.float32)
    tri_gating = jax.nn.sigmoid(
        jnp.dot(flat_rows, tri_gate, preferred_element_type=jnp.float32)
    ).reshape(rows, cols, channels)
    product_normed = layer_norm(product_pairs).astype(jnp.bfloat16)
    tri_update = tri_gating * jnp.dot(
        product_normed.reshape(-1, channels), tri_out, preferred_element_type=jnp.float32
    ).reshape(rows, cols, channels)
    after_tri = (start_pair + tri_update).astype(jnp.bfloat16)
    second = layer_norm(after_tri.astype(jnp.float32)).astype(jnp.bfloat16)
    flat_second = second.reshape(-1, channels)
    query_gate = jnp.dot(flat_second, att_query, preferred_element_type=jnp.float32).reshape(
        rows, cols, 2 * heads_width
    )
    query = (
        (query_gate[..., :heads_width] * HEAD_DIM ** (-0.5))
        .astype(jnp.bfloat16)
        .reshape(rows, cols, HEADS, HEAD_DIM)
    )
    gating = jax.nn.sigmoid(query_gate[..., heads_width:])
    local_bias = (
        jnp.dot(flat_second, att_bias, preferred_element_type=jnp.float32)
        .astype(jnp.bfloat16)
        .reshape(rows, cols, HEADS)
    )
    local_bias = jnp.transpose(local_bias, (2, 0, 1))
    column_all = lax.all_gather(local_bias, "row", axis=1, tiled=True)
    bias_rows = lax.all_to_all(column_all, ("col", "sub"), split_axis=1, concat_axis=2, tiled=True)
    piece = lax.all_gather(second, ("col", "sub"), axis=1, tiled=True)
    width = piece.shape[1]
    keyval = (
        jnp.dot(piece.reshape(-1, channels), att_kv, preferred_element_type=jnp.float32)
        .astype(jnp.bfloat16)
        .reshape(rows, width, 2 * heads_width)
    )
    width = keyval.shape[1]
    key_heads = keyval[..., :heads_width].reshape(rows, width, HEADS, HEAD_DIM)
    value_heads = keyval[..., heads_width:].reshape(rows, width, HEADS, HEAD_DIM)
    scores = jnp.einsum("ijhd,ikhd->ihjk", query, key_heads, preferred_element_type=jnp.float32)
    scores = scores + bias_rows.astype(jnp.float32)[None]
    weights = (jnp.exp(scores) * living).astype(jnp.bfloat16)
    summed = jnp.einsum("ihjk,ikhd->ijhd", weights, value_heads, preferred_element_type=jnp.float32)
    totals = jnp.sum(weights.astype(jnp.float32), axis=3)
    summed, totals = (summed, totals)
    attended = summed / jnp.transpose(totals, (0, 2, 1))[..., None]
    outgoing = (attended.reshape(rows, cols, heads_width) * gating).astype(jnp.bfloat16)
    result = after_tri.astype(jnp.float32) + jnp.dot(
        outgoing.reshape(-1, heads_width), att_out, preferred_element_type=jnp.float32
    ).reshape(rows, cols, channels)
    return result.astype(jnp.bfloat16)


def solution(mesh):
    return jax.shard_map(
        on_device,
        mesh=mesh,
        in_specs=(
            P(("grp", "row"), ("col", "sub"), None),
            P("grp"),
            P("grp"),
            P(),
            P(),
            P(),
            P(),
            P(),
            P(),
            P(),
            P(),
        ),
        out_specs=P(("grp", "row"), ("col", "sub"), None),
        check_vma=False,
    )
```

profile of v0, /device:TPU:25, one launch (start us, length us, event | category | flops | bytes accessed | tf_op | source)
XLA Modules:
  0.0 663.5 jit_solution(13593685487968734741)
XLA Ops:
  8.4 4.4 fusion.24
  12.8 6.2 multiply_reduce_fusion.1
  19.0 4.4 multiply_convert_fusion.2
  23.5 1.3 copy-done.7
  24.8 2.6 fusion.32
  27.4 2.8 fusion.28
  30.2 2.6 maximum_bitcast_fusion
  32.9 8.4 %copy.51 = bf16[2,128,96,96]{3,2,0,1:T(8,128)(2,1)} copy(bf16[2,128,96,96]{1,3,2,0:T(8,128)(2,1)} %maximum_bitcast_fusion) | data formatting | bytes 9437184 | tf_op jit(solution)/shard_map/transpose | solution.py:61
  41.3 140.8 %all_to_all.51 = bf16[2,128,96,96]{3,2,0,1:T(8,128)(2,1)S(1)} all-to-all(bf16[2,128,96,96]{3,2,0,1:T(8,128)(2,1)} %copy.51), channel_id=1, replica_groups=mesh['grp'=2,'row'=4,'col'=2,'sub'=2] {'row'}, dimensions={1} | all-to-all | bytes 9437184 | tf_op jit(solution)/shard_map/all_to_all | solution.py:63
  182.1 4.0 copy.72
  186.2 74.4 %all_to_all.52 = bf16[2,32,384,96]{3,1,0,2:T(8,128)(2,1)} all-to-all(bf16[2,32,384,96]{3,1,0,2:T(8,128)(2,1)S(1)} %bitcast.79), channel_id=1, replica_groups=mesh['grp'=2,'row'=4,'col'=2,'sub'=2] {'col','sub'}, dimensions={2} | all-to-all | bytes 9437184 | tf_op jit(solution)/shard_map/all_to_all | solution.py:62
  260.6 9.7 %copy.73 = bf16[2,32,4,96,96]{3,2,4,1,0:T(4,128)(2,1)} copy(bf16[2,32,4,96,96]{4,1,0,3,2:T(8,128)(2,1)} %bitcast.80) | data formatting | bytes 9437184 | tf_op jit(solution)/shard_map/all_to_all | solution.py:62
  270.3 8.3 %fusion.40 = (bf16[1,32,96,4,96]{2,3,4,1,0:T(4,128)(2,1)}, bf16[1,32,96,4,96]{2,3,4,1,0:T(4,128)(2,1)}) fusion(bf16[2,32,96,4,96]{2,3,4,1,0:T(4,128)(2,1)} %bitcast.77), kind=kLoop, calls=%fused_computation.72 | loop fusion | bytes 9437184 | tf_op jit(solution)/shard_map/slice | solution.py:69
  278.6 7.2 %copy.57 = bf16[1,32,96,4,96]{4,3,2,1,0:T(4,128)(2,1)} copy(bf16[1,32,96,4,96]{2,3,4,1,0:T(4,128)(2,1)} %get-tuple-element.9) | data formatting | bytes 4718592 | tf_op jit(solution)/shard_map/slice | solution.py:69
  285.8 6.0 squeeze.7
  291.8 7.2 %copy.56 = bf16[1,32,96,4,96]{4,3,2,1,0:T(4,128)(2,1)} copy(bf16[1,32,96,4,96]{2,3,4,1,0:T(4,128)(2,1)} %get-tuple-element.10) | data formatting | bytes 4718592 | tf_op jit(solution)/shard_map/slice | solution.py:70
  299.0 6.2 squeeze.6
  305.2 51.8 %all-gather.3.cloned.1.call-done = bf16[32,384,384]{2,1,0:T(8,128)(2,1)} async-done(((bf16[32,96,384]{2,1,0:T(8,128)(2,1)}), bf16[32,384,384]{2,1,0:T(8,128)(2,1)}) %all-gather.3.cloned.1.call-update) | async-done | bytes 9437200 | tf_op jit(solution)/shard_map/all_gather | solution.py:74
  357.0 9.0 %convolution_convert_fusion.2 = bf16[32,96,384]{2,1,0:T(8,128)(2,1)} fusion(bf16[32,96,384]{2,1,0:T(8,128)(2,1)} %squeeze.6, bf16[32,384,384]{2,1,0:T(8,128)(2,1)} %all-gather.3.cloned.1.call-done), kind=kOutput, calls=%fused_computation.53 | convolution fusion | flops 907149312 | bytes 14155776 | tf_op jit(solution)/shard_map/cjk,cik->cji/dot_general | solution.py:71
  366.0 4.9 copy.58
  371.0 4.8 all-to-all-start.2
  376.0 5.3 fusion.2
  381.3 63.0 %all-to-all-done.2 = bf16[32,96,384]{1,0,2:T(8,128)(2,1)} async-done(((bf16[32,96,384]{1,0,2:T(8,128)(2,1)}), bf16[32,96,384]{1,0,2:T(8,128)(2,1)}, u32[]{:S(2)}, u32[]{:S(2)}) %all-to-all-start.2) | async-done | bytes 2359328 | tf_op jit(solution)/shard_map/all_to_all | solution.py:77
  444.3 6.9 %copy.59 = f32[32,96,4,96]{3,1,0,2:T(8,128)} copy(bf16[32,96,4,96]{1,0,3,2:T(8,128)(2,1)} %bitcast.33) | data formatting | bytes 7077888 | tf_op jit(solution)/shard_map/convert_element_type | solution.py:78
  451.1 3.3 bitcast_reduce_fusion
  454.6 3.7 multiply_reduce_fusion
  458.5 5.3 multiply_convert_fusion.1
  463.7 5.2 copy.64
  468.9 5.2 convert_reduce_fusion.1
  474.2 3.2 fusion.5
  477.4 4.2 fusion.6
  481.6 2.5 convolution_convert_fusion.1
  484.3 13.2 %all_gather.11 = bf16[4,384,96]{2,0,1:T(4,128)(2,1)} all-gather(bf16[4,96,96]{2,0,1:T(4,128)(2,1)S(1)} %bitcast.89), channel_id=1, replica_groups=mesh['grp'=2,'row'=4,'col'=2,'sub'=2] {'row'}, dimensions={1}, use_global_device_ids=true | all-gather | bytes 368640 | tf_op jit(solution)/shard_map/all_gather | solution.py:104
  497.5 6.9 %all-to-all-start.3 = ((bf16[4,384,96]{2,0,1:T(4,128)(2,1)}), bf16[4,384,96]{2,0,1:T(4,128)(2,1)S(1)}, u32[]{:S(2)}, u32[]{:S(2)}) async-start(bf16[4,384,96]{2,0,1:T(4,128)(2,1)} %all_gather.11), calls=%async_computation.3 | async-start | bytes 786432 | tf_op jit(solution)/shard_map/all_to_all | solution.py:105
  504.4 1.4 fusion.34
  505.8 3.7 copy-done.4
  510.1 2.8 copy.66
  513.0 2.7 all-to-all-done.3
  516.3 1.2 reshape.165
  517.5 33.5 %all-gather.5.cloned.1.call-done = bf16[96,384,128]{2,1,0:T(8,128)(2,1)} async-done(((bf16[96,96,128]{2,1,0:T(8,128)(2,1)}), bf16[96,384,128]{2,1,0:T(8,128)(2,1)}) %all-gather.5.cloned.1.call-update) | async-done | bytes 9437200 | tf_op jit(solution)/shard_map/all_gather | solution.py:106
  551.1 11.4 %convolution_convert_fusion = bf16[36864,256]{1,0:T(8,128)(2,1)} fusion(bf16[36864,128]{1,0:T(8,128)(2,1)} %bitcast.81, bf16[128,256]{1,0:T(8,128)(2,1)S(1)} %copy-done.10), kind=kOutput, calls=%fused_computation.2 | convolution fusion | flops 2425356288 | bytes 28377088 | tf_op jit(solution)/shard_map/dot_general | solution.py:109
  562.5 14.5 %fusion.39 = (bf16[96,384,128]{2,1,0:T(8,128)(2,1)}, bf16[96,384,128]{2,1,0:T(8,128)(2,1)}) fusion(bf16[96,384,256]{2,1,0:T(8,128)(2,1)} %bitcast.75), kind=kLoop, calls=%fused_computation.71 | loop fusion | bytes 37748736 | tf_op jit(solution)/shard_map/slice | solution.py:115
  577.0 12.6 %copy.65 = bf16[96,384,128]{1,2,0:T(8,128)(2,1)} copy(bf16[96,384,128]{2,1,0:T(8,128)(2,1)} %get-tuple-element.7) | data formatting | bytes 18874368 | tf_op jit(solution)/shard_map/slice | solution.py:115
  589.6 12.7 %copy.67 = bf16[96,384,128]{1,2,0:T(8,128)(2,1)} copy(bf16[96,384,128]{2,1,0:T(8,128)(2,1)} %get-tuple-element.8) | data formatting | bytes 18874368 | tf_op jit(solution)/shard_map/slice | solution.py:114
  602.3 21.6 %convert_reduce_fusion = (f32[96,4,96]{2,1,0:T(4,128)S(1)}, bf16[96,4,96,384]{3,2,1,0:T(8,128)(2,1)}) fusion(f32[384]{0:T(512)S(1)} %convert_element_type.88, f32[4,96,384]{2,1,0:T(8,128)} %reshape.165, bf16[96,96,4,32]{1,3,2,0:T(8,128)(2,1)S(1)} %bitcast.87, bf16[96,384,4,32]{1,3,2,0:T(8,128)(2,1)} %bitcast.83), kind=kOutput, calls=%fused_computation | convolution fusion | flops 976711680 | bytes 40846848 | tf_op jit(solution)/shard_map/ijhd,ikhd->ihjk/dot_general | solution.py:116
  623.9 19.2 %bitcast_divide_fusion = f32[96,96,4,32]{1,3,2,0:T(8,128)} fusion(f32[96,96,4]{1,2,0:T(4,128)S(1)} %bitcast.90, bf16[96,384,4,32]{1,3,2,0:T(8,128)(2,1)} %bitcast.82, bf16[96,4,96,384]{3,2,1,0:T(8,128)(2,1)} %get-tuple-element.18), kind=kOutput, calls=%fused_computation.11 | convolution fusion | flops 907149312 | bytes 42614784 | tf_op jit(solution)/shard_map/ihjk,ikhd->ijhd/dot_general | solution.py:119
  643.1 6.3 copy.70
  649.5 6.7 %fusion.7 = bf16[96,96,128]{2,1,0:T(8,128)(2,1)} fusion(bf16[96,96,128]{2,1,0:T(8,128)(2,1)S(1)} %copy-done.6, f32[96,96,128]{2,1,0:T(8,128)} %copy.70, f32[96,96,256]{2,1,0:T(8,128)} %copy-done.4, bf16[128,128]{1,0:T(8,128)(2,1)S(1)} %copy-done.15), kind=kOutput, calls=%fused_computation.20 | convolution fusion | flops 311427072 | bytes 14188544 | tf_op jit(solution)/shard_map/dot_general | solution.py:124
  (54 shorter events, 4.0 us)
Async XLA Ops:
  6.5 18.3 %copy-start = (bf16[128,512]{1,0:T(8,128)(2,1)S(1)}, bf16[128,512]{1,0:T(8,128)(2,1)}, u32[]{:S(2)}) copy-start(bf16[128,512]{1,0:T(8,128)(2,1)} %param.15) | copy-start | bytes 393220
  6.5 12.4 %copy-start.12 = (f32[128]{0:T(128)S(1)}, f32[128]{0:T(128)}, u32[]{:S(2)}) copy-start(f32[128]{0:T(128)} %param.14) | copy-start | bytes 1540
  6.5 12.4 %copy-start.2 = (bf16[96,96,128]{2,1,0:T(8,128)(2,1)S(1)}, bf16[96,96,128]{2,1,0:T(8,128)(2,1)}, u32[]{:S(2)}) copy-start(bf16[96,96,128]{2,1,0:T(8,128)(2,1)} %param.11) | copy-start | bytes 7077892
  6.5 350.4 %all-gather.3.cloned.1.call-start = ((), (), s32[]{:S(2)}) async-start(), calls=%async_computation.4 | async-start | bytes 11796480 | tf_op jit(solution)/shard_map/all_gather | solution.py:74
  23.4 1.4 copy-start.7
  366.0 10.0 %copy-start.14 = (bf16[128,128]{1,0:T(8,128)(2,1)S(1)}, bf16[128,128]{1,0:T(8,128)(2,1)}, u32[]{:S(2)}) copy-start(bf16[128,128]{1,0:T(8,128)(2,1)} %param.16) | copy-start | bytes 98308
  371.0 73.3 %all-to-all-start.2 = ((bf16[32,96,384]{1,0,2:T(8,128)(2,1)}), bf16[32,96,384]{1,0,2:T(8,128)(2,1)}, u32[]{:S(2)}, u32[]{:S(2)}) async-start(bf16[32,96,384]{1,0,2:T(8,128)(2,1)} %copy.58), calls=%async_computation.2 | async-start | bytes 6291456 | tf_op jit(solution)/shard_map/all_to_all | solution.py:77
  375.8 175.3 %all-gather.5.cloned.1.call-start = ((), (), s32[]{:S(2)}) async-start(), calls=%async_computation.5 | async-start | bytes 11796480 | tf_op jit(solution)/shard_map/all_gather | solution.py:106
  463.7 5.2 copy-start.11
  474.2 3.2 copy-start.5
  474.2 7.4 %copy-start.13 = (bf16[128,4]{0,1:T(4,128)(2,1)S(1)}, bf16[128,4]{0,1:T(4,128)(2,1)}, u32[]{:S(2)}) copy-start(bf16[128,4]{0,1:T(4,128)(2,1)} %param.20) | copy-start | bytes 3076
  477.4 27.0 %copy-start.9 = (bf16[128,256]{1,0:T(8,128)(2,1)S(1)}, bf16[128,256]{1,0:T(8,128)(2,1)}, u32[]{:S(2)}) copy-start(bf16[128,256]{1,0:T(8,128)(2,1)} %param.18) | copy-start | bytes 196612
  481.6 22.8 %copy-start.3 = (bf16[96,96,128]{2,1,0:T(8,128)(2,1)S(1)}, bf16[96,96,128]{2,1,0:T(8,128)(2,1)}, u32[]{:S(2)}) copy-start(bf16[96,96,128]{2,1,0:T(8,128)(2,1)} %fusion.6) | copy-start | bytes 7077892
  497.5 18.2 %all-to-all-start.3 = ((bf16[4,384,96]{2,0,1:T(4,128)(2,1)}), bf16[4,384,96]{2,0,1:T(4,128)(2,1)S(1)}, u32[]{:S(2)}, u32[]{:S(2)}) async-start(bf16[4,384,96]{2,0,1:T(4,128)(2,1)} %all_gather.11), calls=%async_computation.3 | async-start | bytes 786432 | tf_op jit(solution)/shard_map/all_to_all | solution.py:105
  505.8 3.7 copy-start.4
  510.1 41.0 %copy-start.10 = (bf16[128,256]{1,0:T(8,128)(2,1)S(1)}, bf16[128,256]{1,0:T(8,128)(2,1)}, u32[]{:S(2)}) copy-start(bf16[128,256]{1,0:T(8,128)(2,1)} %param.19) | copy-start | bytes 196612
  589.6 12.7 %copy-start.8 = (bf16[96,96,128]{1,2,0:T(8,128)(2,1)S(1)}, bf16[96,96,128]{1,2,0:T(8,128)(2,1)}, u32[]{:S(2)}) copy-start(bf16[96,96,128]{1,2,0:T(8,128)(2,1)} %copy.66) | copy-start | bytes 7077892
  643.1 6.3 copy-start.6
  643.1 6.3 copy-start.15
  649.4 6.7 %copy-start.1 = (bf16[128,512]{1,0:T(8,128)(2,1)S(1)}, bf16[128,512]{1,0:T(8,128)(2,1)}, u32[]{:S(2)}) copy-start(bf16[128,512]{1,0:T(8,128)(2,1)} %param.15) | copy-start | bytes 393220
Sparse Core Ops, SparseCore 0:
  291.9 65.0 all-gather.2
  481.7 69.2 all-gather.4
where the time goes:
time: 675 us; the launch traced here: 663 us
  blocking collectives  228 us (34%)
  waiting for transfers between devices  151 us (22%)
  local copies, waits for them, and re-layouts  131 us (19%)
  matrix products  84.8 us (13%)
  other arithmetic  41.7 us (6%)
  between operations  14.2 us (2%)
  starting transfers between devices  11.9 us (2%)
    all_to_all x1, blocking collectives, on_device(): lax.all_to_all(stacked, 'row', split_axis=1, concat_axis=2, tiled=True)  141 us
    all_to_all x1, blocking collectives, on_device(): lax.all_to_all(lax.all_to_all(stacked, 'row', split_axis=1, concat_axis=2...  74.4 us
    all_to_all x1, waiting for transfers between devices, on_device(): lax.all_to_all(product, 'row', split_axis=2, concat_axis=0, tiled=True)  63 us
    all_gather x1, waiting for transfers between devices, on_device(): lax.all_gather(left_part, ('col', 'sub'), axis=1, tiled=True)  51.8 us
    all_gather x1, waiting for transfers between devices, on_device(): piece = lax.all_gather(second, ('col', 'sub'), axis=1, tiled=True)  33.5 us
    slice x2, local copies, waits for them, and re-layouts, on_device(): keyval[..., heads_width:].reshape(rows, width, HEADS, HEAD_DIM)  27.1 us
    dot_general x1, matrix products, on_device(): jnp.einsum('ijhd,ikhd->ihjk', query, key_heads, preferred_element_type=jn...  21.6 us
    dot_general x1, matrix products, on_device(): jnp.einsum('ihjk,ikhd->ijhd', weights, value_heads, preferred_element_typ...  19.2 us
  transfers between devices with their start and end apart: 4, of which 4 were waited for; matrix products, arithmetic and copies ran while one was open for 4% of the time, Pallas kernels for 0%

commit v1 on v0

--- a/solution.py
+++ b/solution.py
@@ -1,6 +1,10 @@
+import functools
+
 import jax
 import jax.numpy as jnp
 from jax import lax
+from jax.experimental import pallas as pl
+from jax.experimental.pallas import tpu as pltpu
 from jax.sharding import PartitionSpec as P
 
 HEADS = 4
@@ -127,9 +131,318 @@
     return result.astype(jnp.bfloat16)
 
 
+MESH = pl.DeviceIdType.MESH
+F32, BF16 = jnp.float32, jnp.bfloat16
+NT = (((1,), (1,)), ((), ()))
+TN = (((0,), (0,)), ((), ()))
+NN = (((1,), (0,)), ((), ()))
+MASKED = -3.0e38
+VMEM_LIMIT = 60 * 1024 * 1024
+
+
+def gate_of(values):
+    return 0.5 * jnp.tanh(0.5 * values) + 0.5
+
+
+def dot(a, b, dims=NN):
+    return lax.dot_general(a, b, dims, preferred_element_type=F32)
+
+
+def norm_rows(values):
+    average = jnp.mean(values, axis=-1, keepdims=True)
+    centred = values - average
+    spread = jnp.mean(centred * centred, axis=-1, keepdims=True)
+    return centred * lax.rsqrt(spread + EPSILON)
+
+
+def exchange(kernel_id, sizes, everyone, src_of, dst_of, x, out_shape):
+    nr, nc, ns = sizes
+    nq = nc * ns
+    count = nr * nq if everyone else nq
+
+    def kernel(x_ref, y_ref, send_sem, recv_sem, own_sem):
+        q = lax.axis_index("col") * ns + lax.axis_index("sub")
+        me = lax.axis_index("row") * nq + q if everyone else q
+
+        def device(p):
+            where = {"col": lax.rem(p, nq) // ns, "sub": lax.rem(p, ns)}
+            if everyone:
+                where["row"] = p // nq
+            return where
+
+        barrier = pltpu.get_barrier_semaphore()
+        peers = [lax.rem(me + d, count) for d in range(1, count)]
+        for p in peers:
+            pl.semaphore_signal(barrier, inc=1, device_id=device(p), device_id_type=MESH)
+        pl.semaphore_wait(barrier, count - 1)
+        copies = []
+        for d, p in enumerate(peers):
+            copy = pltpu.make_async_remote_copy(
+                src_ref=src_of(x_ref, p),
+                dst_ref=dst_of(y_ref, me),
+                send_sem=send_sem.at[d],
+                recv_sem=recv_sem.at[d],
+                device_id=device(p),
+                device_id_type=MESH,
+            )
+            copy.start()
+            copies.append(copy)
+        own = pltpu.make_async_copy(src_of(x_ref, me), dst_of(y_ref, me), own_sem)
+        own.start()
+        own.wait()
+        for copy in copies:
+            copy.wait()
+
+    return pl.pallas_call(
+        kernel,
+        out_shape=out_shape,
+        in_specs=[pl.BlockSpec(memory_space=pl.ANY)],
+        out_specs=pl.BlockSpec(memory_space=pl.ANY),
+        scratch_shapes=[
+            pltpu.SemaphoreType.DMA((count - 1,)),
+            pltpu.SemaphoreType.DMA((count - 1,)),
+            pltpu.SemaphoreType.DMA,
+        ],
+        compiler_params=pltpu.CompilerParams(collective_id=kernel_id, has_side_effects=True),
+        name="exchange_%d" % kernel_id,
+    )(x)
+
+
+def project_kernel(row_chain, row_live, pair_ref, chain_cols, chain_vec, live_cols, weight, out_ref):
+    i = pl.program_id(0)
+    same = jnp.where(chain_cols[...] == row_chain[i], chain_vec[...], 0.0)
+    normed = norm_rows(pair_ref[0].astype(F32) + same).astype(BF16)
+    half = weight.shape[0] // 2
+    projected = dot(weight[...], normed, NT)
+    mask = live_cols[...] * row_live[i]
+    sides = gate_of(projected[half:]) * projected[:half] * mask
+    groups, wide = out_ref.shape[0], out_ref.shape[2]
+    out_ref[:, 0] = sides.astype(BF16).reshape(groups, wide, sides.shape[1])
+
+
+def product_kernel(count, x_ref, out_ref, *scratch):
+    lanes = x_ref.shape[1] // 128
+    flat, made = scratch[:lanes], scratch[lanes:]
+    total = x_ref.shape[0]
+    wide = 2 * count
+    length = total // wide
+    step = length
+
+    @pl.loop(0, total // step)
+    def _(s):
+        at = pl.ds(pl.multiple_of(s * step, step), step)
+        for t in range(lanes):
+            flat[t][at, :] = x_ref[at, t * 128 : (t + 1) * 128].astype(F32)
+
+    for c in range(count):
+        left = [flat[t][pl.ds(c, length, stride=wide), :].astype(BF16) for t in range(lanes)]
+        right = [flat[t][pl.ds(count + c, length, stride=wide), :].astype(BF16) for t in range(lanes)]
+        product = dot(jnp.concatenate(left, axis=1), jnp.concatenate(right, axis=1), NT)
+        for t in range(lanes):
+            made[t][pl.ds(c, length, stride=count), :] = product[:, t * 128 : (t + 1) * 128]
+
+    @pl.loop(0, out_ref.shape[0] // step)
+    def _(s):
+        at = pl.ds(pl.multiple_of(s * step, step), step)
+        for t in range(lanes):
+            out_ref[at, t * 128 : (t + 1) * 128] = made[t][at, :].astype(BF16)
+
+
+def update_kernel(
+    row_chain, pair_ref, prod_ref, chain_cols, chain_vec, live_cols, tri_gate, tri_out, att_bias,
+    after_ref, second_ref, bias_ref,
+):
+    step = pl.program_id(0)
+    groups, wide, length = prod_ref.shape
+    per = wide // 2
+    both = prod_ref[...].astype(F32)
+    for u in range(2):
+        i = step * 2 + u
+        same = jnp.where(chain_cols[...] == row_chain[i], chain_vec[...], 0.0)
+        start = pair_ref[u].astype(F32) + same
+        normed = norm_rows(start).astype(BF16)
+        gating = gate_of(dot(normed, tri_gate[...]))
+        product = both[:, u * per : (u + 1) * per, :].reshape(groups * per, length)
+        average = jnp.mean(product, axis=0, keepdims=True)
+        centred = product - average
+        spread = jnp.mean(centred * centred, axis=0, keepdims=True)
+        product_normed = (centred * lax.rsqrt(spread + EPSILON)).astype(BF16)
+        after = (start + gating * dot(product_normed, tri_out[...], TN)).astype(BF16)
+        second = norm_rows(after.astype(F32)).astype(BF16)
+        after_ref[u] = after
+        second_ref[u] = second
+        bias = dot(att_bias[...], second, NT)
+        bias = jnp.where(live_cols[...] > 0.0, bias, MASKED)
+        for h in range(HEADS):
+            bias_ref[h, pl.ds(i, 1), :] = bias[h : h + 1, :]
+
+
+def attend_kernel(second_ref, after_ref, bias_ref, att_query, att_kv, att_out, out_ref):
+    width = HEADS * HEAD_DIM
+    second = second_ref[0]
+    query_gate = dot(second, att_query[...])
+    query = (query_gate[:, :width] * HEAD_DIM ** (-0.5)).astype(BF16)
+    gating = gate_of(query_gate[:, width:])
+    keyval = dot(second, att_kv[...]).astype(BF16)
+    key, value = keyval[:, :width], keyval[:, width:]
+    head = lax.broadcasted_iota(jnp.int32, value.shape, 1) // HEAD_DIM
+    summed = None
+    for h in range(HEADS):
+        mine = (head == h).astype(BF16)
+        scores = dot(query * mine, key, NT) + bias_ref[h]
+        weights = jnp.exp(scores).astype(BF16)
+        part = dot(weights, jnp.concatenate([value * mine, mine], axis=1))
+        summed = part if summed is None else summed + part
+    attended = summed[:, :width] / summed[:, width:]
+    outgoing = (attended * gating).astype(BF16)
+    result = after_ref[0].astype(F32) + dot(outgoing, att_out[...])
+    out_ref[0] = result.astype(BF16)
+
+
+def by_rows(
+    sizes,
+    pair,
+    chain_ids,
+    residue_mask,
+    chain_vec,
+    tri_in,
+    tri_gate,
+    tri_out,
+    att_query,
+    att_kv,
+    att_bias,
+    att_out,
+):
+    nr, nc, ns = sizes
+    nq = nc * ns
+    groups = nr * nq
+    rows, cols, channels = pair.shape
+    own = rows // nq
+    length = cols * nq
+    per = channels // groups
+    me = (lax.axis_index("row") * nc + lax.axis_index("col")) * ns + lax.axis_index("sub")
+    living = residue_mask.astype(F32)
+    row_chain = lax.dynamic_slice_in_dim(chain_ids, me * own, own)
+    row_live = lax.dynamic_slice_in_dim(living, me * own, own)
+    chain_cols = jnp.broadcast_to(chain_ids[:, None], (length, channels))
+    live_cols = living[None, :]
+    chain_row = chain_vec[None, :]
+
+    def interleave(a, b):
+        both = jnp.stack([a.T.reshape(groups, per, channels), b.T.reshape(groups, per, channels)], axis=1)
+        return both.reshape(2 * channels, channels)
+
+    quarter = [tri_in[:, n * channels : (n + 1) * channels] for n in range(4)]
+    weight = jnp.concatenate([interleave(quarter[0], quarter[2]), interleave(quarter[1], quarter[3])])
+    bias_weight = jnp.pad(att_bias.T, ((0, 8 - HEADS), (0, 0)))
+
+    pair_rows = exchange(
+        1, sizes, False,
+        lambda x, p: x.at[pl.ds(p * own, own)],
+        lambda y, m: y.at[:, pl.ds(m * cols, cols), :],
+        pair,
+        jax.ShapeDtypeStruct((own, length, channels), BF16),
+    )
+    smem = pl.BlockSpec(memory_space=pltpu.SMEM)
+
+    def whole(*shape):
+        return pl.BlockSpec(shape, lambda s: (0,) * len(shape))
+
+    def row_block(n):
+        return pl.BlockSpec((n, length, channels), lambda s: (s, 0, 0))
+
+    params = pltpu.CompilerParams(vmem_limit_bytes=VMEM_LIMIT)
+    sides = pl.pallas_call(
+        project_kernel,
+        grid=(own,),
+        in_specs=[smem, smem, row_block(1), whole(length, channels), whole(1, channels),
+                  whole(1, length), whole(4 * channels, channels)],
+        out_specs=pl.BlockSpec((groups, 1, 2 * per, length), lambda s: (0, s, 0, 0)),
+        out_shape=jax.ShapeDtypeStruct((groups, own, 2 * per, length), BF16),
+        compiler_params=params,
+        name="project",
+    )(row_chain, row_live, pair_rows, chain_cols, chain_row, live_cols, weight)
+    regrouped = exchange(
+        2, sizes, True, lambda x, p: x.at[p], lambda y, m: y.at[m], sides,
+        jax.ShapeDtypeStruct(sides.shape, BF16),
+    )
+    lanes = length // 128
+    product = pl.pallas_call(
+        functools.partial(product_kernel, per),
+        out_shape=jax.ShapeDtypeStruct((length * per, length), BF16),
+        in_specs=[pl.BlockSpec(memory_space=pltpu.VMEM)],
+        out_specs=pl.BlockSpec(memory_space=pltpu.VMEM),
+        scratch_shapes=[pltpu.VMEM((length * 2 * per, 128), F32)] * lanes
+        + [pltpu.VMEM((length * per, 128), F32)] * lanes,
+        compiler_params=params,
+        name="product",
+    )(regrouped.reshape(length * 2 * per, length))
+    product = product.reshape(groups, own * per, length)
+    returned = exchange(
+        3, sizes, True, lambda x, p: x.at[p], lambda y, m: y.at[m], product,
+        jax.ShapeDtypeStruct(product.shape, BF16),
+    )
+    row_shape = jax.ShapeDtypeStruct((own, length, channels), BF16)
+    after, second, bias = pl.pallas_call(
+        update_kernel,
+        grid=(own // 2,),
+        in_specs=[smem, row_block(2), pl.BlockSpec((groups, 2 * per, length), lambda s: (0, s, 0)),
+                  whole(length, channels), whole(1, channels), whole(1, length),
+                  whole(channels, channels), whole(channels, channels), whole(8, channels)],
+        out_specs=[row_block(2), row_block(2), whole(HEADS, own, length)],
+        out_shape=[row_shape, row_shape, jax.ShapeDtypeStruct((HEADS, own, length), F32)],
+        compiler_params=params,
+        name="update",
+    )(row_chain, pair_rows, returned, chain_cols, chain_row, live_cols, tri_gate, tri_out, bias_weight)
+    bias = bias.astype(BF16).reshape(HEADS * own, length)
+    bias_all = exchange(
+        4, sizes, True, lambda x, p: x, lambda y, m: y.at[m], bias,
+        jax.ShapeDtypeStruct((groups, HEADS * own, length), BF16),
+    )
+    bias_all = jnp.transpose(bias_all.reshape(groups, HEADS, own, length), (1, 0, 2, 3))
+    bias_all = bias_all.reshape(HEADS, length, length).astype(F32)
+    out_rows = pl.pallas_call(
+        attend_kernel,
+        grid=(own,),
+        in_specs=[row_block(1), row_block(1), whole(HEADS, length, length),
+                  whole(channels, 2 * channels), whole(channels, 2 * channels), whole(channels, channels)],
+        out_specs=row_block(1),
+        out_shape=row_shape,
+        compiler_params=params,
+        name="attend",
+    )(second, after, bias_all, att_query, att_kv, att_out)
+    return exchange(
+        5, sizes, False,
+        lambda x, p: x.at[:, pl.ds(p * cols, cols), :],
+        lambda y, m: y.at[pl.ds(m * own, own)],
+        out_rows,
+        jax.ShapeDtypeStruct((rows, cols, channels), BF16),
+    )
+
+
+def device_program(sizes, pair, *rest):
+    rows, cols, channels = pair.shape
+    nr, nc, ns = sizes
+    nq = nc * ns
+    length = cols * nq
+    fits = (
+        rows % (2 * nq) == 0
+        and (rows // nq) % 8 == 0
+        and cols % 16 == 0
+        and channels == 128
+        and channels == 8 * nr * nq
+        and length % 128 == 0
+        and length == rows * nr
+    )
+    if fits:
+        return by_rows(sizes, pair, *rest)
+    return on_device(pair, *rest)
+
+
 def solution(mesh):
+    sizes = tuple(mesh.shape[name] for name in ("row", "col", "sub"))
     return jax.shard_map(
-        on_device,
+        functools.partial(device_program, sizes),
         mesh=mesh,
         in_specs=(
             P(("grp", "row"), ("col", "sub"), None),

time: 675 us -> 347 us (0.51); the launches traced: 663 us -> 345 us
  Pallas kernels: 0 us -> 331 us
  blocking collectives: 228 us -> 0 us
  waiting for transfers between devices: 151 us -> 0 us
  local copies, waits for them, and re-layouts: 131 us -> 11.3 us
  matrix products: 84.8 us -> 0 us
  other arithmetic: 41.7 us -> 2.92 us
  between operations: 14.2 us -> 0.12 us
  starting transfers between devices: 11.9 us -> 0 us
    pallas_call x0 -> x9, Pallas kernels: none -> 331 us  [the longest x5 248 us: exchange(): pl.pallas_call(kernel, out_shape=out_shape, in_specs=[pl.BlockSpec(memory...]
    all_to_all x2 -> x0, blocking collectives: 215 us -> none  [the longest x1 141 us: on_device(): lax.all_to_all(stacked, 'row', split_axis=1, concat_axis=2, tiled=True)]
    all_gather x2 -> x0, waiting for transfers between devices: 85.3 us -> none  [the longest x1 51.8 us: on_device(): lax.all_gather(left_part, ('col', 'sub'), axis=1, tiled=True)]
    dot_general x10 -> x0, matrix products: 84.8 us -> none  [the longest x1 21.6 us: on_device(): jnp.einsum('ijhd,ikhd->ihjk', query, key_heads, preferred_element_type=jn...]
    all_to_all x2 -> x0, waiting for transfers between devices: 65.8 us -> none  [the longest x1 63 us: on_device(): lax.all_to_all(product, 'row', split_axis=2, concat_axis=0, tiled=True)]
    slice x6 -> x1, local copies, waits for them, and re-layouts: 62.6 us -> 0.82 us  [by_rows(): quarter = [tri_in[:, n * channels:(n + 1) * channels] for n in range(4)]]
    reduce_sum x5 -> x0, other arithmetic: 20.6 us -> none  [the longest x3 13 us: layer_norm(): spread = jnp.mean(centred * centred, axis=-1, keepdims=True)]
    convert_element_type x6 -> x1, local copies, waits for them, and re-layouts: 21.6 us -> 2.84 us  [by_rows(): bias_all = bias_all.reshape(HEADS, length, length).astype(F32)]
  transfers between devices with their start and end apart: 4 -> 0, of which waited for: 4 -> 0; matrix products, arithmetic and copies ran while one was open for 4% -> 0% of each run, Pallas kernels for 0% -> 0%
where the time goes in v1:
time: 347 us; the launch traced here: 345 us
  Pallas kernels  331 us (95%)
  local copies, waits for them, and re-layouts  11.3 us (3%)
    pallas_call x5, Pallas kernels, exchange(): pl.pallas_call(kernel, out_shape=out_shape, in_specs=[pl.BlockSpec(memory...  248 us
    pallas_call x1, Pallas kernels, by_rows(): pl.pallas_call(attend_kernel, grid=(own,), in_specs=[row_block(1), row_bl...  37 us
    pallas_call x1, Pallas kernels, by_rows(): pl.pallas_call(project_kernel, grid=(own,), in_specs=[smem, smem, row_blo...  19.1 us
    pallas_call x1, Pallas kernels, by_rows(): pl.pallas_call(update_kernel, grid=(own // 2,), in_specs=[smem, row_block...  18 us
    pallas_call x1, Pallas kernels, by_rows(): pl.pallas_call(functools.partial(product_kernel, per), out_shape=jax.Shap...  8.65 us

profile of v1, /device:TPU:25, one launch (start us, length us, event | category | flops | bytes accessed | tf_op | source)
XLA Modules:
  0.0 345.0 jit_solution(17057007804636776002)
XLA Ops:
  0.0 0.7 convert_element_type.17
  0.7 0.6 dynamic_slice.7.row_live
  1.3 1.3 dynamic_slice.6.row_chain
  2.6 0.8 fusion
  3.5 0.1 copy.26
  3.6 0.1 copy.27
  3.8 0.1 copy.24
  3.9 0.1 copy.25
  4.0 0.7 pad_maximum_fusion.weight
  4.7 0.6 broadcast_in_dim.14.live_cols
  5.3 0.0 copy-start
  5.3 28.6 %exchange_1.1.pair_ref = bf16[24,384,128]{2,1,0:T(8,128)(2,1)} custom-call(bf16[96,96,128]{2,1,0:T(8,128)(2,1)} %x_ref.1), custom_call_target="tpu_custom_call" | custom-call | tf_op jit(solution)/shard_map/exchange_1/pallas_call | solution.py:196
  33.9 0.0 copy-done
  33.9 0.8 broadcast_in_dim.12.chain_cols
  34.7 19.1 %project.1.x_ref = bf16[16,24,16,384]{3,2,1,0:T(8,128)(2,1)} custom-call(s32[24]{0:T(128)} %dynamic_slice.6.row_chain, f32[24]{0:T(128)} %dynamic_slice.7.row_live, bf16[24,384,128]{2,1,0:T(8,128)(2,1)} %exchange_1.1.pair_ref, s32[384,128]{1,0:T(8,128)} %broadcast_in_dim.12.chain_cols, f32[1,128]{1,0:T(1,128)} %bitcast.35, ...), custom_call_target="tpu_custom_call" | custom-call | tf_op jit(solution)/shard_map/project/pallas_call | solution.py:355
  53.8 94.0 %exchange_2.1 = bf16[16,24,16,384]{3,2,1,0:T(8,128)(2,1)} custom-call(bf16[16,24,16,384]{3,2,1,0:T(8,128)(2,1)} %project.1.x_ref), custom_call_target="tpu_custom_call" | custom-call | tf_op jit(solution)/shard_map/exchange_2/pallas_call | solution.py:196
  147.7 8.7 %product.1 = bf16[3072,384]{1,0:T(8,128)(2,1)} custom-call(bf16[6144,384]{1,0:T(8,128)(2,1)} %bitcast.24), custom_call_target="tpu_custom_call" | custom-call | tf_op jit(solution)/shard_map/product/pallas_call | solution.py:370
  156.4 0.0 copy-start.1
  156.4 61.7 %exchange_3.1.prod_ref = bf16[16,192,384]{2,1,0:T(8,128)(2,1)} custom-call(bf16[16,192,384]{2,1,0:T(8,128)(2,1)} %bitcast.25), custom_call_target="tpu_custom_call" | custom-call | tf_op jit(solution)/shard_map/exchange_3/pallas_call | solution.py:196
  218.1 0.0 copy-done.1
  218.1 0.6 pad.4.att_bias
  218.7 18.0 %update.1 = (bf16[24,384,128]{2,1,0:T(8,128)(2,1)}, bf16[24,384,128]{2,1,0:T(8,128)(2,1)}, f32[4,24,384]{2,1,0:T(8,128)}) custom-call(s32[24]{0:T(128)} %dynamic_slice.6.row_chain, bf16[24,384,128]{2,1,0:T(8,128)(2,1)} %exchange_1.1.pair_ref, bf16[16,192,384]{2,1,0:T(8,128)(2,1)} %exchange_3.1.prod_ref, s32[384,128]{1,0:T(8,128)} %broadcast_in_dim.12.chain_cols, ...), custom_call_target="tpu_custom_call" | custom-call | tf_op jit(solution)/shard_map/update/pallas_call | solution.py:386
  236.8 1.6 convert_element_type.18
  238.3 33.3 %exchange_4.1 = bf16[16,96,384]{2,1,0:T(8,128)(2,1)} custom-call(bf16[96,384]{1,0:T(8,128)(2,1)} %bitcast.28), custom_call_target="tpu_custom_call" | custom-call | tf_op jit(solution)/shard_map/exchange_4/pallas_call | solution.py:196
  271.6 2.8 copy.23
  274.4 37.0 %attend.1.x_ref = bf16[24,384,128]{2,1,0:T(8,128)(2,1)} custom-call(bf16[24,384,128]{2,1,0:T(8,128)(2,1)} %get-tuple-element.8.second_ref, bf16[24,384,128]{2,1,0:T(8,128)(2,1)} %get-tuple-element.9.after_ref, f32[4,384,384]{2,1,0:T(8,128)} %bitcast.26, bf16[128,256]{1,0:T(8,128)(2,1)} %att_query.1, bf16[128,256]{1,0:T(8,128)(2,1)} %att_kv.1, ...), custom_call_target="tpu_custom_call" | custom-call | tf_op jit(solution)/shard_map/attend/pallas_call | solution.py:404
  311.5 30.3 %exchange_5.1 = bf16[96,96,128]{2,1,0:T(8,128)(2,1)} custom-call(bf16[24,384,128]{2,1,0:T(8,128)(2,1)} %attend.1.x_ref), custom_call_target="tpu_custom_call" | custom-call | tf_op jit(solution)/shard_map/exchange_5/pallas_call | solution.py:196
  341.8 3.2 copy.29
  (4 shorter events, 0.0 us)
Async XLA Ops:
  5.3 28.6 %copy-start = (s32[384]{0:T(512)S(1)}, s32[384]{0:T(512)}, u32[]{:S(2)}) copy-start(s32[384]{0:T(512)} %param.12) | copy-start | bytes 4612
  156.4 61.7 %copy-start.1 = (bf16[128,4]{0,1:T(4,128)(2,1)S(1)}, bf16[128,4]{0,1:T(4,128)(2,1)}, u32[]{:S(2)}) copy-start(bf16[128,4]{0,1:T(4,128)(2,1)} %param.20) | copy-start | bytes 3076

commit v2 on v0

--- a/solution.py
+++ b/solution.py
@@ -1,6 +1,10 @@
+import functools
+
 import jax
 import jax.numpy as jnp
 from jax import lax
+from jax.experimental import pallas as pl
+from jax.experimental.pallas import tpu as pltpu
 from jax.sharding import PartitionSpec as P
 
 HEADS = 4
@@ -127,9 +131,435 @@
     return result.astype(jnp.bfloat16)
 
 
+MESH = pl.DeviceIdType.MESH
+F32, BF16 = jnp.float32, jnp.bfloat16
+NT = (((1,), (1,)), ((), ()))
+TN = (((0,), (0,)), ((), ()))
+NN = (((1,), (0,)), ((), ()))
+MASKED = -3.0e38
+VMEM_LIMIT = 60 * 1024 * 1024
+
+
+def gate_of(values):
+    return 0.5 * jnp.tanh(0.5 * values) + 0.5
+
+
+def dot(a, b, dims=NN):
+    return lax.dot_general(a, b, dims, preferred_element_type=F32)
+
+
+def norm_rows(values):
+    average = jnp.mean(values, axis=-1, keepdims=True)
+    centred = values - average
+    spread = jnp.mean(centred * centred, axis=-1, keepdims=True)
+    return centred * lax.rsqrt(spread + EPSILON)
+
+
+CHUNK = 4
+
+
+def position(sizes):
+    nr, nc, ns = sizes
+    r = lax.axis_index("row")
+    q = lax.axis_index("col") * ns + lax.axis_index("sub")
+
+    def device(row, place):
+        return {"row": row, "col": place // ns, "sub": lax.rem(place, ns)}
+
+    return r, q, device
+
+
+def peers_of(sizes):
+    nr, nc, ns = sizes
+    nq = nc * ns
+    r, q, device = position(sizes)
+    found = []
+    for d in range(1, nr * nq):
+        dr, dq = d // nq, d % nq
+        row, place = lax.rem(r + dr, nr), lax.rem(q + dq, nq)
+        found.append((row * nq + place, device(row, place)))
+    return found
+
+
+def meet(devices):
+    barrier = pltpu.get_barrier_semaphore()
+    for where in devices:
+        pl.semaphore_signal(barrier, inc=1, device_id=where, device_id_type=MESH)
+    pl.semaphore_wait(barrier, len(devices))
+
+
+def send(src, dst, send_sem, recv_sem, where):
+    copy = pltpu.make_async_remote_copy(
+        src_ref=src, dst_ref=dst, send_sem=send_sem, recv_sem=recv_sem,
+        device_id=where, device_id_type=MESH,
+    )
+    copy.start()
+    return copy
+
+
+def project_kernel(
+    sizes, row_chain, row_live, chain_cols, chain_vec, live_cols, weight, pair_ref,
+    rows_ref, grouped_ref, sides, in_send, in_recv, in_own, out_send, out_recv, out_own,
+):
+    nr, nc, ns = sizes
+    nq = nc * ns
+    r, q, device = position(sizes)
+    me = r * nq + q
+    groups, own, wide, length = sides.shape
+    cols = length // nq
+    chunks = own // CHUNK
+    half = weight.shape[0] // 2
+    peers = peers_of(sizes)
+    meet([where for _, where in peers])
+    arriving = []
+    for n in range(chunks):
+        some = pl.ds(n * CHUNK, CHUNK)
+        here = pl.ds(q * cols, cols)
+        now = []
+        for d in range(1, nq):
+            p = lax.rem(q + d, nq)
+            now.append(send(
+                pair_ref.at[pl.ds(p * own + n * CHUNK, CHUNK)], rows_ref.at[some, here, :],
+                in_send.at[n, d - 1], in_recv.at[n, d - 1], device(r, p),
+            ))
+        mine = pltpu.make_async_copy(
+            pair_ref.at[pl.ds(q * own + n * CHUNK, CHUNK)], rows_ref.at[some, here, :], in_own.at[n]
+        )
+        mine.start()
+        arriving.append((now, mine))
+    leaving = []
+    for n in range(chunks):
+        now, mine = arriving[n]
+        mine.wait()
+        for copy in now:
+            copy.wait_recv()
+
+        @pl.loop(n * CHUNK, (n + 1) * CHUNK)
+        def _(i):
+            same = jnp.where(chain_cols[...] == row_chain[i], chain_vec[...], 0.0)
+            normed = norm_rows(rows_ref[i].astype(F32) + same).astype(BF16)
+            projected = dot(weight[...], normed, NT)
+            mask = live_cols[...] * row_live[i]
+            both = gate_of(projected[half:]) * projected[:half] * mask
+            sides[:, i] = both.astype(BF16).reshape(groups, wide, length)
+
+        some = pl.ds(n * CHUNK, CHUNK)
+        for d, (p, where) in enumerate(peers):
+            leaving.append(send(
+                sides.at[p, some], grouped_ref.at[me, some], out_send.at[n, d], out_recv.at[n, d], where
+            ))
+        mine = pltpu.make_async_copy(sides.at[me, some], grouped_ref.at[me, some], out_own.at[n])
+        mine.start()
+        leaving.append(mine)
+    for now, _ in arriving:
+        for copy in now:
+            copy.wait_send()
+    for copy in leaving:
+        copy.wait()
+
+
+def product_kernel(count, x_ref, out_ref, *scratch):
+    lanes = x_ref.shape[1] // 128
+    flat, made = scratch[:lanes], scratch[lanes:]
+    total = x_ref.shape[0]
+    wide = 2 * count
+    length = total // wide
+    step = length
+
+    @pl.loop(0, total // step)
+    def _(s):
+        at = pl.ds(pl.multiple_of(s * step, step), step)
+        for t in range(lanes):
+            flat[t][at, :] = x_ref[at, t * 128 : (t + 1) * 128].astype(F32)
+
+    for c in range(count):
+        left = [flat[t][pl.ds(c, length, stride=wide), :].astype(BF16) for t in range(lanes)]
+        right = [flat[t][pl.ds(count + c, length, stride=wide), :].astype(BF16) for t in range(lanes)]
+        product = dot(jnp.concatenate(left, axis=1), jnp.concatenate(right, axis=1), NT)
+        for t in range(lanes):
+            made[t][pl.ds(c, length, stride=count), :] = product[:, t * 128 : (t + 1) * 128]
+
+    @pl.loop(0, out_ref.shape[0] // step)
+    def _(s):
+        at = pl.ds(pl.multiple_of(s * step, step), step)
+        for t in range(lanes):
+            out_ref[at, t * 128 : (t + 1) * 128] = made[t][at, :].astype(BF16)
+
+
+def update_kernel(
+    sizes, row_chain, pair_ref, prod_ref, chain_cols, chain_vec, live_cols, tri_gate, tri_out, att_bias,
+    after_ref, second_ref, gathered, landed, bias_ref, bias_out,
+    in_send, in_recv, in_own, row_send, row_recv, col_send, col_recv, sub_send, sub_recv, own_sem,
+):
+    nr, nc, ns = sizes
+    nq = nc * ns
+    r, q, device = position(sizes)
+    c, u = lax.axis_index("col"), lax.axis_index("sub")
+    me = r * nq + q
+    groups, tall, length = landed.shape
+    own = pair_ref.shape[0]
+    per = tall // own
+    chunks = own // CHUNK
+    peers = peers_of(sizes)
+    meet([where for _, where in peers])
+    arriving = []
+    for n in range(chunks):
+        some = pl.ds(n * CHUNK * per, CHUNK * per)
+        now = [
+            send(prod_ref.at[p, some], landed.at[me, some], in_send.at[n, d], in_recv.at[n, d], where)
+            for d, (p, where) in enumerate(peers)
+        ]
+        mine = pltpu.make_async_copy(prod_ref.at[me, some], landed.at[me, some], in_own.at[n])
+        mine.start()
+        arriving.append((now, mine))
+    for n in range(chunks):
+        now, mine = arriving[n]
+        mine.wait()
+        for copy in now:
+            copy.wait_recv()
+
+        @pl.loop(n * CHUNK // 2, (n + 1) * CHUNK // 2)
+        def _(step):
+            at = pl.ds(pl.multiple_of(step * 2 * per, 2 * per), 2 * per)
+            both = landed[:, at, :].astype(F32)
+            for v in range(2):
+                i = step * 2 + v
+                same = jnp.where(chain_cols[...] == row_chain[i], chain_vec[...], 0.0)
+                start = pair_ref[i].astype(F32) + same
+                normed = norm_rows(start).astype(BF16)
+                gating = gate_of(dot(normed, tri_gate[...]))
+                product = both[:, v * per : (v + 1) * per, :].reshape(groups * per, length)
+                average = jnp.mean(product, axis=0, keepdims=True)
+                centred = product - average
+                spread = jnp.mean(centred * centred, axis=0, keepdims=True)
+                product_normed = (centred * lax.rsqrt(spread + EPSILON)).astype(BF16)
+                after = (start + gating * dot(product_normed, tri_out[...], TN)).astype(BF16)
+                second = norm_rows(after.astype(F32)).astype(BF16)
+                after_ref[i] = after
+                second_ref[i] = second
+                bias = dot(att_bias[...], second, NT)
+                bias = jnp.where(live_cols[...] > 0.0, bias, MASKED)
+                for h in range(HEADS):
+                    bias_ref[pl.ds(h * own + i, 1), :] = bias[h : h + 1, :]
+
+    bias_out[...] = bias_ref[...].astype(BF16)
+    mine = pltpu.make_async_copy(bias_out, gathered.at[q, r], own_sem)
+    mine.start()
+    hops = []
+    for d in range(1, nr):
+        hops.append(send(
+            bias_out, gathered.at[q, r], row_send.at[d - 1], row_recv.at[d - 1],
+            device(lax.rem(r + d, nr), q),
+        ))
+    mine.wait()
+    for copy in hops:
+        copy.wait_recv()
+    across = []
+    for d in range(1, nc):
+        across.append(send(
+            gathered.at[q], gathered.at[q], col_send.at[d - 1], col_recv.at[d - 1],
+            device(r, lax.rem(c + d, nc) * ns + u),
+        ))
+    last = []
+
+    def pass_on(e):
+        source = lax.rem(c + nc - e, nc) * ns + u
+        for d in range(1, ns):
+            last.append(send(
+                gathered.at[source], gathered.at[source], sub_send.at[e, d - 1], sub_recv.at[e, d - 1],
+                device(r, c * ns + lax.rem(u + d, ns)),
+            ))
+
+    pass_on(0)
+    for e, copy in enumerate(across):
+        copy.wait_recv()
+        pass_on(e + 1)
+    for copy in last:
+        copy.wait()
+    for copy in hops + across:
+        copy.wait_send()
+    for now, _ in arriving:
+        for copy in now:
+            copy.wait_send()
+
+
+def attend_kernel(
+    sizes, second_ref, after_ref, bias_ref, att_query, att_kv, att_out,
+    out_ref, made, out_send, out_recv, out_own,
+):
+    nr, nc, ns = sizes
+    nq = nc * ns
+    r, q, device = position(sizes)
+    own, length, width = made.shape
+    cols = length // nq
+    others = [lax.rem(q + d, nq) for d in range(1, nq)]
+    meet([device(r, p) for p in others])
+    head = lax.broadcasted_iota(jnp.int32, (length, width), 1) // HEAD_DIM
+    leaving = []
+    for n in range(own // CHUNK):
+
+        @pl.loop(n * CHUNK, (n + 1) * CHUNK)
+        def _(i):
+            second = second_ref[i]
+            query_gate = dot(second, att_query[...])
+            query = (query_gate[:, :width] * HEAD_DIM ** (-0.5)).astype(BF16)
+            gating = gate_of(query_gate[:, width:])
+            keyval = dot(second, att_kv[...]).astype(BF16)
+            key, value = keyval[:, :width], keyval[:, width:]
+            summed = None
+            for h in range(HEADS):
+                mine = (head == h).astype(BF16)
+                scores = dot(query * mine, key, NT) + bias_ref[h]
+                weights = jnp.exp(scores).astype(BF16)
+                part = dot(weights, jnp.concatenate([value * mine, mine], axis=1))
+                summed = part if summed is None else summed + part
+            attended = summed[:, :width] / summed[:, width:]
+            outgoing = (attended * gating).astype(BF16)
+            result = after_ref[i].astype(F32) + dot(outgoing, att_out[...])
+            made[i] = result.astype(BF16)
+
+        some = pl.ds(n * CHUNK, CHUNK)
+        to = pl.ds(q * own + n * CHUNK, CHUNK)
+        for d, p in enumerate(others):
+            leaving.append(send(
+                made.at[some, pl.ds(p * cols, cols), :], out_ref.at[to],
+                out_send.at[n, d], out_recv.at[n, d], device(r, p),
+            ))
+        mine = pltpu.make_async_copy(made.at[some, pl.ds(q * cols, cols), :], out_ref.at[to], out_own.at[n])
+        mine.start()
+        leaving.append(mine)
+    for copy in leaving:
+        copy.wait()
+
+
+def by_rows(
+    sizes,
+    pair,
+    chain_ids,
+    residue_mask,
+    chain_vec,
+    tri_in,
+    tri_gate,
+    tri_out,
+    att_query,
+    att_kv,
+    att_bias,
+    att_out,
+):
+    nr, nc, ns = sizes
+    nq = nc * ns
+    groups = nr * nq
+    rows, cols, channels = pair.shape
+    own = rows // nq
+    length = cols * nq
+    per = channels // groups
+    me = (lax.axis_index("row") * nc + lax.axis_index("col")) * ns + lax.axis_index("sub")
+    living = residue_mask.astype(F32)
+    row_chain = lax.dynamic_slice_in_dim(chain_ids, me * own, own)
+    row_live = lax.dynamic_slice_in_dim(living, me * own, own)
+    chain_cols = jnp.broadcast_to(chain_ids[:, None], (length, channels))
+    live_cols = living[None, :]
+    chain_row = chain_vec[None, :]
+
+    def interleave(a, b):
+        both = jnp.stack([a.T.reshape(groups, per, channels), b.T.reshape(groups, per, channels)], axis=1)
+        return both.reshape(2 * channels, channels)
+
+    quarter = [tri_in[:, n * channels : (n + 1) * channels] for n in range(4)]
+    weight = jnp.concatenate([interleave(quarter[0], quarter[2]), interleave(quarter[1], quarter[3])])
+    bias_weight = jnp.pad(att_bias.T, ((0, 8 - HEADS), (0, 0)))
+
+    chunks = own // CHUNK
+    smem = pl.BlockSpec(memory_space=pltpu.SMEM)
+    vmem = pl.BlockSpec(memory_space=pltpu.VMEM)
+    anywhere = pl.BlockSpec(memory_space=pl.ANY)
+    dma = pltpu.SemaphoreType.DMA
+    row_shape = jax.ShapeDtypeStruct((own, length, channels), BF16)
+
+    def params(n):
+        return pltpu.CompilerParams(collective_id=n, has_side_effects=True, vmem_limit_bytes=VMEM_LIMIT)
+
+    side_shape = (groups, own, 2 * per, length)
+    pair_rows, regrouped = pl.pallas_call(
+        functools.partial(project_kernel, sizes),
+        in_specs=[smem, smem, vmem, vmem, vmem, vmem, anywhere],
+        out_specs=[vmem, anywhere],
+        out_shape=[row_shape, jax.ShapeDtypeStruct(side_shape, BF16)],
+        scratch_shapes=[
+            pltpu.VMEM(side_shape, BF16),
+            dma((chunks, nq - 1)), dma((chunks, nq - 1)), dma((chunks,)),
+            dma((chunks, groups - 1)), dma((chunks, groups - 1)), dma((chunks,)),
+        ],
+        compiler_params=params(1),
+        name="project",
+    )(row_chain, row_live, chain_cols, chain_row, live_cols, weight, pair)
+    lanes = length // 128
+    product = pl.pallas_call(
+        functools.partial(product_kernel, per),
+        out_shape=jax.ShapeDtypeStruct((length * per, length), BF16),
+        in_specs=[vmem],
+        out_specs=vmem,
+        scratch_shapes=[pltpu.VMEM((length * 2 * per, 128), F32)] * lanes
+        + [pltpu.VMEM((length * per, 128), F32)] * lanes,
+        compiler_params=pltpu.CompilerParams(vmem_limit_bytes=VMEM_LIMIT),
+        name="product",
+    )(regrouped.reshape(length * 2 * per, length))
+    product = product.reshape(groups, own * per, length)
+    tall = HEADS * own
+    after, second, bias_all = pl.pallas_call(
+        functools.partial(update_kernel, sizes),
+        in_specs=[smem, vmem, anywhere, vmem, vmem, vmem, vmem, vmem, vmem],
+        out_specs=[vmem, vmem, vmem],
+        out_shape=[row_shape, row_shape, jax.ShapeDtypeStruct((nq, nr, tall, length), BF16)],
+        scratch_shapes=[
+            pltpu.VMEM(product.shape, BF16), pltpu.VMEM((tall, length), F32), pltpu.VMEM((tall, length), BF16),
+            dma((chunks, groups - 1)), dma((chunks, groups - 1)), dma((chunks,)),
+            dma((max(nr - 1, 1),)), dma((max(nr - 1, 1),)),
+            dma((max(nc - 1, 1),)), dma((max(nc - 1, 1),)),
+            dma((nc, max(ns - 1, 1))), dma((nc, max(ns - 1, 1))), dma,
+        ],
+        compiler_params=params(2),
+        name="update",
+    )(row_chain, pair_rows, product, chain_cols, chain_row, live_cols, tri_gate, tri_out, bias_weight)
+    bias_all = jnp.transpose(bias_all.reshape(nq, nr, HEADS, own, length), (2, 1, 0, 3, 4))
+    bias_all = bias_all.reshape(HEADS, length, length).astype(F32)
+    return pl.pallas_call(
+        functools.partial(attend_kernel, sizes),
+        in_specs=[vmem] * 6,
+        out_specs=anywhere,
+        out_shape=jax.ShapeDtypeStruct((rows, cols, channels), BF16),
+        scratch_shapes=[
+            pltpu.VMEM(row_shape.shape, BF16),
+            dma((chunks, nq - 1)), dma((chunks, nq - 1)), dma((chunks,)),
+        ],
+        compiler_params=params(3),
+        name="attend",
+    )(second, after, bias_all, att_query, att_kv, att_out)
+
+
+def device_program(sizes, pair, *rest):
+    rows, cols, channels = pair.shape
+    nr, nc, ns = sizes
+    nq = nc * ns
+    length = cols * nq
+    fits = (
+        rows % (2 * nq) == 0
+        and (rows // nq) % 8 == 0
+        and cols % 16 == 0
+        and channels == 128
+        and channels == 8 * nr * nq
+        and length % 128 == 0
+        and length == rows * nr
+    )
+    if fits:
+        return by_rows(sizes, pair, *rest)
+    return on_device(pair, *rest)
+
+
 def solution(mesh):
+    sizes = tuple(mesh.shape[name] for name in ("row", "col", "sub"))
     return jax.shard_map(
-        on_device,
+        functools.partial(device_program, sizes),
         mesh=mesh,
         in_specs=(
             P(("grp", "row"), ("col", "sub"), None),

time: 675 us -> 268 us (0.40); the launches traced: 663 us -> 267 us
  Pallas kernels: 0 us -> 253 us
  blocking collectives: 228 us -> 0 us
  waiting for transfers between devices: 151 us -> 0 us
  local copies, waits for them, and re-layouts: 131 us -> 12.8 us
  matrix products: 84.8 us -> 0 us
  other arithmetic: 41.7 us -> 1.37 us
  between operations: 14.2 us -> 0.09 us
  starting transfers between devices: 11.9 us -> 0 us
    pallas_call x0 -> x4, Pallas kernels: none -> 253 us  [the longest x1 118 us: by_rows(): pl.pallas_call(functools.partial(project_kernel, sizes), in_specs=[smem,...]
    all_to_all x2 -> x0, blocking collectives: 215 us -> none  [the longest x1 141 us: on_device(): lax.all_to_all(stacked, 'row', split_axis=1, concat_axis=2, tiled=True)]
    all_gather x2 -> x0, waiting for transfers between devices: 85.3 us -> none  [the longest x1 51.8 us: on_device(): lax.all_gather(left_part, ('col', 'sub'), axis=1, tiled=True)]
    dot_general x10 -> x0, matrix products: 84.8 us -> none  [the longest x1 21.6 us: on_device(): jnp.einsum('ijhd,ikhd->ihjk', query, key_heads, preferred_element_type=jn...]
    all_to_all x2 -> x0, waiting for transfers between devices: 65.8 us -> none  [the longest x1 63 us: on_device(): lax.all_to_all(product, 'row', split_axis=2, concat_axis=0, tiled=True)]
    slice x6 -> x1, local copies, waits for them, and re-layouts: 62.6 us -> 0.82 us  [by_rows(): quarter = [tri_in[:, n * channels:(n + 1) * channels] for n in range(4)]]
    reduce_sum x5 -> x0, other arithmetic: 20.6 us -> none  [the longest x3 13 us: layer_norm(): spread = jnp.mean(centred * centred, axis=-1, keepdims=True)]
    convert_element_type x6 -> x1, local copies, waits for them, and re-layouts: 21.6 us -> 2.93 us  [by_rows(): bias_all = bias_all.reshape(HEADS, length, length).astype(F32)]
  transfers between devices with their start and end apart: 4 -> 0, of which waited for: 4 -> 0; matrix products, arithmetic and copies ran while one was open for 4% -> 0% of each run, Pallas kernels for 0% -> 0%
where the time goes in v2:
time: 268 us; the launch traced here: 267 us
  Pallas kernels  253 us (94%)
  local copies, waits for them, and re-layouts  12.8 us (5%)
    pallas_call x1, Pallas kernels, by_rows(): pl.pallas_call(functools.partial(project_kernel, sizes), in_specs=[smem,...  118 us
    pallas_call x1, Pallas kernels, by_rows(): pl.pallas_call(functools.partial(update_kernel, sizes), in_specs=[smem, v...  82.3 us
    pallas_call x1, Pallas kernels, by_rows(): pl.pallas_call(functools.partial(attend_kernel, sizes), in_specs=[vmem] *...  44.2 us
    pallas_call x1, Pallas kernels, by_rows(): pl.pallas_call(functools.partial(product_kernel, per), out_shape=jax.Shap...  8.65 us

profile of v2, /device:TPU:25, one launch (start us, length us, event | category | flops | bytes accessed | tf_op | source)
XLA Modules:
  0.0 267.5 jit_solution(18008768495194736759)
XLA Ops:
  0.0 1.3 dynamic_slice.6.row_chain
  1.3 0.7 convert_element_type.14
  2.0 0.7 dynamic_slice.7.row_live
  2.6 0.6 broadcast_in_dim.14.live_cols
  3.2 1.3 pad.4.att_bias
  4.5 0.8 fusion
  5.3 0.1 copy.24
  5.4 0.1 copy.26
  5.6 0.1 copy.25
  5.7 0.1 copy.27
  5.9 0.7 pad_maximum_fusion.weight
  6.5 1.5 broadcast_in_dim.12.chain_cols
  8.0 118.1 %project.1 = (bf16[24,384,128]{2,1,0:T(8,128)(2,1)}, bf16[16,24,16,384]{3,2,1,0:T(8,128)(2,1)}) custom-call(s32[24]{0:T(128)} %dynamic_slice.6.row_chain, f32[24]{0:T(128)} %dynamic_slice.7.row_live, s32[384,128]{1,0:T(8,128)} %broadcast_in_dim.12.chain_cols, f32[1,128]{1,0:T(1,128)} %bitcast.33, f32[1,384]{1,0:T(1,128)} %broadcast_in_dim.14.live_cols, ...), custom_call_target="tpu_custom_call" | custom-call | tf_op jit(solution)/shard_map/project/pallas_call | solution.py:483
  126.2 8.7 %product.1 = bf16[3072,384]{1,0:T(8,128)(2,1)} custom-call(bf16[6144,384]{1,0:T(8,128)(2,1)} %bitcast.25), custom_call_target="tpu_custom_call" | custom-call | tf_op jit(solution)/shard_map/product/pallas_call | solution.py:497
  134.8 82.3 %update.1 = (bf16[24,384,128]{2,1,0:T(8,128)(2,1)}, bf16[24,384,128]{2,1,0:T(8,128)(2,1)}, bf16[4,4,96,384]{3,2,1,0:T(8,128)(2,1)}) custom-call(s32[24]{0:T(128)} %dynamic_slice.6.row_chain, bf16[24,384,128]{2,1,0:T(8,128)(2,1)} %get-tuple-element.10.pair_ref, bf16[16,192,384]{2,1,0:T(8,128)(2,1)} %bitcast.23, s32[384,128]{1,0:T(8,128)} %broadcast_in_dim.12.chain_cols, ...), custom_call_target="tpu_custom_call" | custom-call | tf_op jit(solution)/shard_map/update/pallas_call | solution.py:509
  217.1 2.9 %copy.23 = f32[4,4,4,24,384]{4,3,0,1,2:T(8,128)} copy(bf16[4,4,4,24,384]{4,3,2,1,0:T(8,128)(2,1)} %bitcast.26) | data formatting | bytes 3538944 | tf_op jit(solution)/shard_map/convert_element_type | solution.py:525
  220.0 44.2 %attend.1 = bf16[96,96,128]{2,1,0:T(8,128)(2,1)} custom-call(bf16[24,384,128]{2,1,0:T(8,128)(2,1)} %get-tuple-element.12.second_ref, bf16[24,384,128]{2,1,0:T(8,128)(2,1)} %get-tuple-element.13.after_ref, f32[4,384,384]{2,1,0:T(8,128)} %bitcast.24, bf16[128,256]{1,0:T(8,128)(2,1)} %att_query.1, bf16[128,256]{1,0:T(8,128)(2,1)} %att_kv.1, ...), custom_call_target="tpu_custom_call" | custom-call | tf_op jit(solution)/shard_map/attend/pallas_call | solution.py:526
  264.3 3.2 %copy.29 = bf16[96,96,128]{2,1,0:T(8,128)(2,1)} copy(bf16[96,96,128]{2,1,0:T(8,128)(2,1)} %attend.1) | data formatting | bytes 4718592
  (4 shorter events, 0.0 us)

commit v3 on v2

--- a/solution.py
+++ b/solution.py
@@ -172,13 +172,23 @@
 def peers_of(sizes):
     nr, nc, ns = sizes
     nq = nc * ns
+    deep = nr // 2
     r, q, device = position(sizes)
+    half, z = r // deep, lax.rem(r, deep)
     found = []
-    for d in range(1, nr * nq):
-        dr, dq = d // nq, d % nq
-        row, place = lax.rem(r + dr, nr), lax.rem(q + dq, nq)
-        found.append((row * nq + place, device(row, place)))
+    for e in range(2):
+        for d in range(deep):
+            for o in range(nq):
+                if e or d or o:
+                    level, place = lax.rem(z + d, deep), lax.rem(q + o, nq)
+                    row = lax.rem(half + e, 2) * deep + level
+                    found.append((level * nq + place, row * nq + place, device(row, place), e == 0))
     return found
+
+
+def columns_of(ids):
+    spread = jnp.broadcast_to(ids.astype(F32), (128, ids.shape[1]))
+    return spread.T.astype(jnp.int32)
 
 
 def meet(devices):
@@ -198,19 +208,22 @@
 
 
 def project_kernel(
-    sizes, row_chain, row_live, chain_cols, chain_vec, live_cols, weight, pair_ref,
-    rows_ref, grouped_ref, sides, in_send, in_recv, in_own, out_send, out_recv, out_own,
+    sizes, chain_ids, residue_mask, chain_row, live_row, chain_vec, weight, pair_ref,
+    rows_ref, left_ref, right_ref, left, right, chain_cols,
+    in_send, in_recv, in_own, left_send, left_recv, right_send, right_recv, out_own,
 ):
     nr, nc, ns = sizes
     nq = nc * ns
     r, q, device = position(sizes)
     me = r * nq + q
-    groups, own, wide, length = sides.shape
+    mine_in_half = lax.rem(r, nr // 2) * nq + q
+    groups, own, wide, length = left.shape
     cols = length // nq
     chunks = own // CHUNK
     half = weight.shape[0] // 2
+    side = half // 2
     peers = peers_of(sizes)
-    meet([where for _, where in peers])
+    meet([peer[2] for peer in peers])
     arriving = []
     for n in range(chunks):
         some = pl.ds(n * CHUNK, CHUNK)
@@ -227,6 +240,8 @@
         )
         mine.start()
         arriving.append((now, mine))
+    chain_cols[...] = columns_of(chain_row[...])
+    live_cols = live_row[...].astype(F32)
     leaving = []
     for n in range(chunks):
         now, mine = arriving[n]
@@ -236,21 +251,34 @@
 
         @pl.loop(n * CHUNK, (n + 1) * CHUNK)
         def _(i):
-            same = jnp.where(chain_cols[...] == row_chain[i], chain_vec[...], 0.0)
+            at = me * own + i
+            same = jnp.where(chain_cols[...] == chain_ids[at], chain_vec[...], 0.0)
             normed = norm_rows(rows_ref[i].astype(F32) + same).astype(BF16)
             projected = dot(weight[...], normed, NT)
-            mask = live_cols[...] * row_live[i]
-            both = gate_of(projected[half:]) * projected[:half] * mask
-            sides[:, i] = both.astype(BF16).reshape(groups, wide, length)
+            mask = live_cols * residue_mask[at].astype(F32)
+            both = (gate_of(projected[half:]) * projected[:half] * mask).astype(BF16)
+            left[:, i] = both[:side].reshape(groups, wide, length)
+            right[:, i] = both[side:].reshape(groups, wide, length)
 
         some = pl.ds(n * CHUNK, CHUNK)
-        for d, (p, where) in enumerate(peers):
+        near = 0
+        for d, (p, _, where, same_half) in enumerate(peers):
             leaving.append(send(
-                sides.at[p, some], grouped_ref.at[me, some], out_send.at[n, d], out_recv.at[n, d], where
+                right.at[p, some], right_ref.at[me, some], right_send.at[n, d], right_recv.at[n, d], where
             ))
-        mine = pltpu.make_async_copy(sides.at[me, some], grouped_ref.at[me, some], out_own.at[n])
-        mine.start()
-        leaving.append(mine)
+            if same_half:
+                leaving.append(send(
+                    left.at[p, some], left_ref.at[mine_in_half, some],
+                    left_send.at[n, near], left_recv.at[n, near], where,
+                ))
+                near += 1
+        for k, (a, b) in enumerate((
+            (left.at[mine_in_half, some], left_ref.at[mine_in_half, some]),
+            (right.at[mine_in_half, some], right_ref.at[me, some]),
+        )):
+            mine = pltpu.make_async_copy(a, b, out_own.at[n, k])
+            mine.start()
+            leaving.append(mine)
     for now, _ in arriving:
         for copy in now:
             copy.wait_send()
@@ -258,26 +286,26 @@
         copy.wait()
 
 
-def product_kernel(count, x_ref, out_ref, *scratch):
-    lanes = x_ref.shape[1] // 128
-    flat, made = scratch[:lanes], scratch[lanes:]
-    total = x_ref.shape[0]
-    wide = 2 * count
-    length = total // wide
-    step = length
-
-    @pl.loop(0, total // step)
-    def _(s):
-        at = pl.ds(pl.multiple_of(s * step, step), step)
+def product_kernel(count, left_ref, right_ref, out_ref, *scratch):
+    lanes = left_ref.shape[1] // 128
+    left, right, made = scratch[:lanes], scratch[lanes : 2 * lanes], scratch[2 * lanes :]
+    step = left_ref.shape[1]
+    for source, flat in ((left_ref, left), (right_ref, right)):
+
+        @pl.loop(0, source.shape[0] // step)
+        def _(s):
+            at = pl.ds(pl.multiple_of(s * step, step), step)
+            for t in range(lanes):
+                flat[t][at, :] = source[at, t * 128 : (t + 1) * 128].astype(F32)
+
+    def channel(flat, c):
+        at = pl.ds(c, flat[0].shape[0] // count, stride=count)
+        return jnp.concatenate([part[at, :].astype(BF16) for part in flat], axis=1)
+
+    for c in range(count):
+        product = dot(channel(left, c), channel(right, c), NT)
         for t in range(lanes):
-            flat[t][at, :] = x_ref[at, t * 128 : (t + 1) * 128].astype(F32)
-
-    for c in range(count):
-        left = [flat[t][pl.ds(c, length, stride=wide), :].astype(BF16) for t in range(lanes)]
-        right = [flat[t][pl.ds(count + c, length, stride=wide), :].astype(BF16) for t in range(lanes)]
-        product = dot(jnp.concatenate(left, axis=1), jnp.concatenate(right, axis=1), NT)
-        for t in range(lanes):
-            made[t][pl.ds(c, length, stride=count), :] = product[:, t * 128 : (t + 1) * 128]
+            made[t][pl.ds(c, product.shape[0], stride=count), :] = product[:, t * 128 : (t + 1) * 128]
 
     @pl.loop(0, out_ref.shape[0] // step)
     def _(s):
@@ -287,8 +315,8 @@
 
 
 def update_kernel(
-    sizes, row_chain, pair_ref, prod_ref, chain_cols, chain_vec, live_cols, tri_gate, tri_out, att_bias,
-    after_ref, second_ref, gathered, landed, bias_ref, bias_out,
+    sizes, chain_ids, pair_ref, prod_ref, chain_row, live_row, chain_vec, tri_gate, tri_out, att_bias,
+    after_ref, second_ref, gathered, landed, bias_ref, bias_out, chain_cols,
     in_send, in_recv, in_own, row_send, row_recv, col_send, col_recv, sub_send, sub_recv, own_sem,
 ):
     nr, nc, ns = sizes
@@ -296,51 +324,53 @@
     r, q, device = position(sizes)
     c, u = lax.axis_index("col"), lax.axis_index("sub")
     me = r * nq + q
+    mine_in_half = lax.rem(r, nr // 2) * nq + q
     groups, tall, length = landed.shape
     own = pair_ref.shape[0]
     per = tall // own
     chunks = own // CHUNK
-    peers = peers_of(sizes)
-    meet([where for _, where in peers])
+    near = [peer for peer in peers_of(sizes) if peer[3]]
+    meet([peer[2] for peer in peers_of(sizes)])
     arriving = []
     for n in range(chunks):
         some = pl.ds(n * CHUNK * per, CHUNK * per)
         now = [
-            send(prod_ref.at[p, some], landed.at[me, some], in_send.at[n, d], in_recv.at[n, d], where)
-            for d, (p, where) in enumerate(peers)
+            send(prod_ref.at[p, some], landed.at[mine_in_half, some], in_send.at[n, d], in_recv.at[n, d], where)
+            for d, (p, _, where, _) in enumerate(near)
         ]
-        mine = pltpu.make_async_copy(prod_ref.at[me, some], landed.at[me, some], in_own.at[n])
+        mine = pltpu.make_async_copy(
+            prod_ref.at[mine_in_half, some], landed.at[mine_in_half, some], in_own.at[n]
+        )
         mine.start()
         arriving.append((now, mine))
+    chain_cols[...] = columns_of(chain_row[...])
+    live_cols = live_row[...].astype(F32)
     for n in range(chunks):
         now, mine = arriving[n]
         mine.wait()
         for copy in now:
             copy.wait_recv()
 
-        @pl.loop(n * CHUNK // 2, (n + 1) * CHUNK // 2)
-        def _(step):
-            at = pl.ds(pl.multiple_of(step * 2 * per, 2 * per), 2 * per)
-            both = landed[:, at, :].astype(F32)
-            for v in range(2):
-                i = step * 2 + v
-                same = jnp.where(chain_cols[...] == row_chain[i], chain_vec[...], 0.0)
-                start = pair_ref[i].astype(F32) + same
-                normed = norm_rows(start).astype(BF16)
-                gating = gate_of(dot(normed, tri_gate[...]))
-                product = both[:, v * per : (v + 1) * per, :].reshape(groups * per, length)
-                average = jnp.mean(product, axis=0, keepdims=True)
-                centred = product - average
-                spread = jnp.mean(centred * centred, axis=0, keepdims=True)
-                product_normed = (centred * lax.rsqrt(spread + EPSILON)).astype(BF16)
-                after = (start + gating * dot(product_normed, tri_out[...], TN)).astype(BF16)
-                second = norm_rows(after.astype(F32)).astype(BF16)
-                after_ref[i] = after
-                second_ref[i] = second
-                bias = dot(att_bias[...], second, NT)
-                bias = jnp.where(live_cols[...] > 0.0, bias, MASKED)
-                for h in range(HEADS):
-                    bias_ref[pl.ds(h * own + i, 1), :] = bias[h : h + 1, :]
+        @pl.loop(n * CHUNK, (n + 1) * CHUNK)
+        def _(i):
+            at = pl.ds(pl.multiple_of(i * per, per), per)
+            product = landed[:, at, :].astype(F32).reshape(groups * per, length)
+            same = jnp.where(chain_cols[...] == chain_ids[me * own + i], chain_vec[...], 0.0)
+            start = pair_ref[i].astype(F32) + same
+            normed = norm_rows(start).astype(BF16)
+            gating = gate_of(dot(normed, tri_gate[...]))
+            average = jnp.mean(product, axis=0, keepdims=True)
+            centred = product - average
+            spread = jnp.mean(centred * centred, axis=0, keepdims=True)
+            product_normed = (centred * lax.rsqrt(spread + EPSILON)).astype(BF16)
+            after = (start + gating * dot(product_normed, tri_out[...], TN)).astype(BF16)
+            second = norm_rows(after.astype(F32)).astype(BF16)
+            after_ref[i] = after
+            second_ref[i] = second
+            bias = dot(att_bias[...], second, NT)
+            bias = jnp.where(live_cols > 0.0, bias, MASKED)
+            for h in range(HEADS):
+                bias_ref[pl.ds(h * own + i, 1), :] = bias[h : h + 1, :]
 
     bias_out[...] = bias_ref[...].astype(BF16)
     mine = pltpu.make_async_copy(bias_out, gathered.at[q, r], own_sem)
@@ -452,21 +482,11 @@
     rows, cols, channels = pair.shape
     own = rows // nq
     length = cols * nq
-    per = channels // groups
-    me = (lax.axis_index("row") * nc + lax.axis_index("col")) * ns + lax.axis_index("sub")
-    living = residue_mask.astype(F32)
-    row_chain = lax.dynamic_slice_in_dim(chain_ids, me * own, own)
-    row_live = lax.dynamic_slice_in_dim(living, me * own, own)
-    chain_cols = jnp.broadcast_to(chain_ids[:, None], (length, channels))
-    live_cols = living[None, :]
-    chain_row = chain_vec[None, :]
-
-    def interleave(a, b):
-        both = jnp.stack([a.T.reshape(groups, per, channels), b.T.reshape(groups, per, channels)], axis=1)
-        return both.reshape(2 * channels, channels)
-
-    quarter = [tri_in[:, n * channels : (n + 1) * channels] for n in range(4)]
-    weight = jnp.concatenate([interleave(quarter[0], quarter[2]), interleave(quarter[1], quarter[3])])
+    near = groups // 2
+    per = channels // near
+    chain_row, live_row, chain_one = chain_ids[None, :], residue_mask[None, :], chain_vec[None, :]
+    order = [tri_in[:, n * channels : (n + 1) * channels] for n in (0, 2, 1, 3)]
+    weight = jnp.concatenate(order, axis=1).T
     bias_weight = jnp.pad(att_bias.T, ((0, 8 - HEADS), (0, 0)))
 
     chunks = own // CHUNK
@@ -479,32 +499,39 @@
     def params(n):
         return pltpu.CompilerParams(collective_id=n, has_side_effects=True, vmem_limit_bytes=VMEM_LIMIT)
 
-    side_shape = (groups, own, 2 * per, length)
-    pair_rows, regrouped = pl.pallas_call(
+    side_shape = (near, own, per, length)
+    pair_rows, left, right = pl.pallas_call(
         functools.partial(project_kernel, sizes),
         in_specs=[smem, smem, vmem, vmem, vmem, vmem, anywhere],
-        out_specs=[vmem, anywhere],
-        out_shape=[row_shape, jax.ShapeDtypeStruct(side_shape, BF16)],
+        out_specs=[vmem, anywhere, anywhere],
+        out_shape=[
+            row_shape,
+            jax.ShapeDtypeStruct(side_shape, BF16),
+            jax.ShapeDtypeStruct((groups, own, per, length), BF16),
+        ],
         scratch_shapes=[
-            pltpu.VMEM(side_shape, BF16),
+            pltpu.VMEM(side_shape, BF16), pltpu.VMEM(side_shape, BF16), pltpu.VMEM((length, channels), jnp.int32),
             dma((chunks, nq - 1)), dma((chunks, nq - 1)), dma((chunks,)),
-            dma((chunks, groups - 1)), dma((chunks, groups - 1)), dma((chunks,)),
+            dma((chunks, near - 1)), dma((chunks, near - 1)),
+            dma((chunks, groups - 1)), dma((chunks, groups - 1)), dma((chunks, 2)),
         ],
         compiler_params=params(1),
         name="project",
-    )(row_chain, row_live, chain_cols, chain_row, live_cols, weight, pair)
+    )(chain_ids, residue_mask, chain_row, live_row, chain_one, weight, pair)
     lanes = length // 128
+    tall_left, tall_right = near * own * per, length * per
     product = pl.pallas_call(
         functools.partial(product_kernel, per),
-        out_shape=jax.ShapeDtypeStruct((length * per, length), BF16),
-        in_specs=[vmem],
+        out_shape=jax.ShapeDtypeStruct((tall_left, length), BF16),
+        in_specs=[vmem, vmem],
         out_specs=vmem,
-        scratch_shapes=[pltpu.VMEM((length * 2 * per, 128), F32)] * lanes
-        + [pltpu.VMEM((length * per, 128), F32)] * lanes,
+        scratch_shapes=[pltpu.VMEM((tall_left, 128), F32)] * lanes
+        + [pltpu.VMEM((tall_right, 128), F32)] * lanes
+        + [pltpu.VMEM((tall_left, 128), F32)] * lanes,
         compiler_params=pltpu.CompilerParams(vmem_limit_bytes=VMEM_LIMIT),
         name="product",
-    )(regrouped.reshape(length * 2 * per, length))
-    product = product.reshape(groups, own * per, length)
+    )(left.reshape(tall_left, length), right.reshape(tall_right, length))
+    product = product.reshape(near, own * per, length)
     tall = HEADS * own
     after, second, bias_all = pl.pallas_call(
         functools.partial(update_kernel, sizes),
@@ -513,14 +540,15 @@
         out_shape=[row_shape, row_shape, jax.ShapeDtypeStruct((nq, nr, tall, length), BF16)],
         scratch_shapes=[
             pltpu.VMEM(product.shape, BF16), pltpu.VMEM((tall, length), F32), pltpu.VMEM((tall, length), BF16),
-            dma((chunks, groups - 1)), dma((chunks, groups - 1)), dma((chunks,)),
+            pltpu.VMEM((length, channels), jnp.int32),
+            dma((chunks, near - 1)), dma((chunks, near - 1)), dma((chunks,)),
             dma((max(nr - 1, 1),)), dma((max(nr - 1, 1),)),
             dma((max(nc - 1, 1),)), dma((max(nc - 1, 1),)),
             dma((nc, max(ns - 1, 1))), dma((nc, max(ns - 1, 1))), dma,
         ],
         compiler_params=params(2),
         name="update",
-    )(row_chain, pair_rows, product, chain_cols, chain_row, live_cols, tri_gate, tri_out, bias_weight)
+    )(chain_ids, pair_rows, product, chain_row, live_row, chain_one, tri_gate, tri_out, bias_weight)
     bias_all = jnp.transpose(bias_all.reshape(nq, nr, HEADS, own, length), (2, 1, 0, 3, 4))
     bias_all = bias_all.reshape(HEADS, length, length).astype(F32)
     return pl.pallas_call(
@@ -547,6 +575,7 @@
         and (rows // nq) % 8 == 0
         and cols % 16 == 0
         and channels == 128
+        and nr % 2 == 0
         and channels == 8 * nr * nq
         and length % 128 == 0
         and length == rows * nr

time: 268 us -> 253 us (0.944)
  Pallas kernels: 253 us -> 241 us
    pallas_call x1, Pallas kernels: 82.3 us -> 57.4 us  [by_rows(): pl.pallas_call(functools.partial(update_kernel, sizes), in_specs=[smem, v...]
    pallas_call x1, Pallas kernels: 118 us -> 126 us  [by_rows(): pl.pallas_call(functools.partial(project_kernel, sizes), in_specs=[smem,...]
    pallas_call x1, Pallas kernels: 8.65 us -> 13.4 us  [by_rows(): pl.pallas_call(functools.partial(product_kernel, per), out_shape=jax.Shap...]
where the time goes in v3:
time: 253 us
  Pallas kernels  241 us (95%)
  local copies, waits for them, and re-layouts  10.6 us (4%)
    pallas_call x1, Pallas kernels, by_rows(): pl.pallas_call(functools.partial(project_kernel, sizes), in_specs=[smem,...  126 us
    pallas_call x1, Pallas kernels, by_rows(): pl.pallas_call(functools.partial(update_kernel, sizes), in_specs=[smem, v...  57.4 us
    pallas_call x1, Pallas kernels, by_rows(): pl.pallas_call(functools.partial(attend_kernel, sizes), in_specs=[vmem] *...  44.2 us
    pallas_call x1, Pallas kernels, by_rows(): pl.pallas_call(functools.partial(product_kernel, per), out_shape=jax.Shap...  13.4 us

profile of v3, /device:TPU:25, one launch (start us, length us, event | category | flops | bytes accessed | tf_op | source)
XLA Modules:
  0.0 252.6 jit_solution(16338838516487636172)
XLA Ops:
  0.0 1.3 broadcast_in_dim.9.chain_row
  1.3 1.3 broadcast_in_dim.10.live_row
  2.5 0.8 fusion
  3.3 0.1 copy.20
  3.5 0.1 copy.19
  3.6 0.1 copy.18
  3.7 0.1 copy.17
  3.8 0.7 maximum_bitcast_fusion.weight
  4.5 126.3 %project.1 = (bf16[24,384,128]{2,1,0:T(8,128)(2,1)}, bf16[8,24,16,384]{3,2,1,0:T(8,128)(2,1)}, bf16[16,24,16,384]{3,2,1,0:T(8,128)(2,1)}) custom-call(s32[384]{0:T(512)} %chain_ids.3, s32[384]{0:T(512)} %residue_mask.1, s32[1,384]{1,0:T(1,128)} %broadcast_in_dim.9.chain_row, s32[1,384]{1,0:T(1,128)} %broadcast_in_dim.10.live_row, f32[1,128]{1,0:T(1,128)} %bitcast.17, ...), custom_call_target="tpu_custom_call" | custom-call | tf_op jit(solution)/shard_map/project/pallas_call | solution.py:503
  130.9 0.0 copy-start
  130.9 13.4 %product.1 = bf16[3072,384]{1,0:T(8,128)(2,1)} custom-call(bf16[3072,384]{1,0:T(8,128)(2,1)} %bitcast.15, bf16[6144,384]{1,0:T(8,128)(2,1)} %bitcast.14), custom_call_target="tpu_custom_call" | custom-call | tf_op jit(solution)/shard_map/product/pallas_call | solution.py:523
  144.2 0.0 copy-done
  144.2 0.6 pad.4.att_bias
  144.8 57.4 %update.1 = (bf16[24,384,128]{2,1,0:T(8,128)(2,1)}, bf16[24,384,128]{2,1,0:T(8,128)(2,1)}, bf16[4,4,96,384]{3,2,1,0:T(8,128)(2,1)}) custom-call(s32[384]{0:T(512)} %chain_ids.3, bf16[24,384,128]{2,1,0:T(8,128)(2,1)} %get-tuple-element.11.pair_ref, bf16[8,384,384]{2,1,0:T(8,128)(2,1)} %bitcast.12, s32[1,384]{1,0:T(1,128)} %broadcast_in_dim.9.chain_row, ...), custom_call_target="tpu_custom_call" | custom-call | tf_op jit(solution)/shard_map/update/pallas_call | solution.py:536
  202.2 2.9 %copy.16 = f32[4,4,4,24,384]{4,3,0,1,2:T(8,128)} copy(bf16[4,4,4,24,384]{4,3,2,1,0:T(8,128)(2,1)} %bitcast.16) | data formatting | bytes 3538944 | tf_op jit(solution)/shard_map/convert_element_type | solution.py:553
  205.1 44.2 %attend.1 = bf16[96,96,128]{2,1,0:T(8,128)(2,1)} custom-call(bf16[24,384,128]{2,1,0:T(8,128)(2,1)} %get-tuple-element.14.second_ref, bf16[24,384,128]{2,1,0:T(8,128)(2,1)} %get-tuple-element.15.after_ref, f32[4,384,384]{2,1,0:T(8,128)} %bitcast.13, bf16[128,256]{1,0:T(8,128)(2,1)} %att_query.1, bf16[128,256]{1,0:T(8,128)(2,1)} %att_kv.1, ...), custom_call_target="tpu_custom_call" | custom-call | tf_op jit(solution)/shard_map/attend/pallas_call | solution.py:554
  249.3 3.2 %copy.22 = bf16[96,96,128]{2,1,0:T(8,128)(2,1)} copy(bf16[96,96,128]{2,1,0:T(8,128)(2,1)} %attend.1) | data formatting | bytes 4718592
Async XLA Ops:
  130.9 13.4 %copy-start = (bf16[128,4]{0,1:T(4,128)(2,1)S(1)}, bf16[128,4]{0,1:T(4,128)(2,1)}, u32[]{:S(2)}) copy-start(bf16[128,4]{0,1:T(4,128)(2,1)} %param.20) | copy-start | bytes 3076

commit v4 on v3

--- a/solution.py
+++ b/solution.py
@@ -286,7 +286,7 @@
         copy.wait()
 
 
-def product_kernel(count, left_ref, right_ref, out_ref, *scratch):
+def multiply(count, left_ref, right_ref, out_ref, scratch):
     lanes = left_ref.shape[1] // 128
     left, right, made = scratch[:lanes], scratch[lanes : 2 * lanes], scratch[2 * lanes :]
     step = left_ref.shape[1]
@@ -307,17 +307,22 @@
         for t in range(lanes):
             made[t][pl.ds(c, product.shape[0], stride=count), :] = product[:, t * 128 : (t + 1) * 128]
 
-    @pl.loop(0, out_ref.shape[0] // step)
-    def _(s):
-        at = pl.ds(pl.multiple_of(s * step, step), step)
+    tall = out_ref.shape[1]
+
+    @pl.loop(0, out_ref.shape[0])
+    def _(g):
+        at = pl.ds(pl.multiple_of(g * tall, tall), tall)
         for t in range(lanes):
-            out_ref[at, t * 128 : (t + 1) * 128] = made[t][at, :].astype(BF16)
-
-
-def update_kernel(
-    sizes, chain_ids, pair_ref, prod_ref, chain_row, live_row, chain_vec, tri_gate, tri_out, att_bias,
-    after_ref, second_ref, gathered, landed, bias_ref, bias_out, chain_cols,
+            out_ref[g, :, t * 128 : (t + 1) * 128] = made[t][at, :].astype(BF16)
+
+
+def finish_kernel(
+    sizes, chain_ids, left_ref, right_ref, pair_ref, chain_row, live_row, chain_vec, tri_gate, tri_out, att_bias,
+    att_query, att_kv, att_out,
+    out_ref, prod_ref, landed, bias_ref, bias_out, chain_cols, gathered, bias_full,
+    after_ref, second_ref, query_ref, key_ref, value_ref, made,
     in_send, in_recv, in_own, row_send, row_recv, col_send, col_recv, sub_send, sub_recv, own_sem,
+    out_send, out_recv, out_own, *flat,
 ):
     nr, nc, ns = sizes
     nq = nc * ns
@@ -329,8 +334,12 @@
     own = pair_ref.shape[0]
     per = tall // own
     chunks = own // CHUNK
+    width = HEADS * HEAD_DIM
+    cols = length // nq
     near = [peer for peer in peers_of(sizes) if peer[3]]
+    others = [lax.rem(q + d, nq) for d in range(1, nq)]
     meet([peer[2] for peer in peers_of(sizes)])
+    multiply(per, left_ref, right_ref, prod_ref, flat)
     arriving = []
     for n in range(chunks):
         some = pl.ds(n * CHUNK * per, CHUNK * per)
@@ -381,6 +390,18 @@
             bias_out, gathered.at[q, r], row_send.at[d - 1], row_recv.at[d - 1],
             device(lax.rem(r + d, nr), q),
         ))
+
+    def prepare(first, past):
+        @pl.loop(first, past)
+        def _(i):
+            second = second_ref[i]
+            query = dot(second, att_query[:, :width])
+            query_ref[i] = (query * HEAD_DIM ** (-0.5)).astype(BF16)
+            keyval = dot(second, att_kv[...]).astype(BF16)
+            key_ref[i] = keyval[:, :width]
+            value_ref[i] = keyval[:, width:]
+
+    prepare(0, own // 2)
     mine.wait()
     for copy in hops:
         copy.wait_recv()
@@ -401,6 +422,7 @@
             ))
 
     pass_on(0)
+    prepare(own // 2, own)
     for e, copy in enumerate(across):
         copy.wait_recv()
         pass_on(e + 1)
@@ -411,19 +433,11 @@
     for now, _ in arriving:
         for copy in now:
             copy.wait_send()
-
-
-def attend_kernel(
-    sizes, second_ref, after_ref, bias_ref, att_query, att_kv, att_out,
-    out_ref, made, out_send, out_recv, out_own,
-):
-    nr, nc, ns = sizes
-    nq = nc * ns
-    r, q, device = position(sizes)
-    own, length, width = made.shape
-    cols = length // nq
-    others = [lax.rem(q + d, nq) for d in range(1, nq)]
-    meet([device(r, p) for p in others])
+    for row in range(nr):
+        for place in range(nq):
+            block = gathered[place, row].astype(F32)
+            for h in range(HEADS):
+                bias_full[h, (row * nq + place) * own : (row * nq + place + 1) * own, :] = block[h * own : (h + 1) * own]
     head = lax.broadcasted_iota(jnp.int32, (length, width), 1) // HEAD_DIM
     leaving = []
     for n in range(own // CHUNK):
@@ -431,15 +445,12 @@
         @pl.loop(n * CHUNK, (n + 1) * CHUNK)
         def _(i):
             second = second_ref[i]
-            query_gate = dot(second, att_query[...])
-            query = (query_gate[:, :width] * HEAD_DIM ** (-0.5)).astype(BF16)
-            gating = gate_of(query_gate[:, width:])
-            keyval = dot(second, att_kv[...]).astype(BF16)
-            key, value = keyval[:, :width], keyval[:, width:]
+            gating = gate_of(dot(second, att_query[:, width:]))
+            query, key, value = query_ref[i], key_ref[i], value_ref[i]
             summed = None
             for h in range(HEADS):
                 mine = (head == h).astype(BF16)
-                scores = dot(query * mine, key, NT) + bias_ref[h]
+                scores = dot(query * mine, key, NT) + bias_full[h]
                 weights = jnp.exp(scores).astype(BF16)
                 part = dot(weights, jnp.concatenate([value * mine, mine], axis=1))
                 summed = part if summed is None else summed + part
@@ -520,49 +531,34 @@
     )(chain_ids, residue_mask, chain_row, live_row, chain_one, weight, pair)
     lanes = length // 128
     tall_left, tall_right = near * own * per, length * per
-    product = pl.pallas_call(
-        functools.partial(product_kernel, per),
-        out_shape=jax.ShapeDtypeStruct((tall_left, length), BF16),
-        in_specs=[vmem, vmem],
-        out_specs=vmem,
-        scratch_shapes=[pltpu.VMEM((tall_left, 128), F32)] * lanes
-        + [pltpu.VMEM((tall_right, 128), F32)] * lanes
-        + [pltpu.VMEM((tall_left, 128), F32)] * lanes,
-        compiler_params=pltpu.CompilerParams(vmem_limit_bytes=VMEM_LIMIT),
-        name="product",
-    )(left.reshape(tall_left, length), right.reshape(tall_right, length))
-    product = product.reshape(near, own * per, length)
     tall = HEADS * own
-    after, second, bias_all = pl.pallas_call(
-        functools.partial(update_kernel, sizes),
-        in_specs=[smem, vmem, anywhere, vmem, vmem, vmem, vmem, vmem, vmem],
-        out_specs=[vmem, vmem, vmem],
-        out_shape=[row_shape, row_shape, jax.ShapeDtypeStruct((nq, nr, tall, length), BF16)],
+    rows_bf16 = pltpu.VMEM(row_shape.shape, BF16)
+    return pl.pallas_call(
+        functools.partial(finish_kernel, sizes),
+        in_specs=[smem] + [vmem] * 12,
+        out_specs=anywhere,
+        out_shape=jax.ShapeDtypeStruct((rows, cols, channels), BF16),
         scratch_shapes=[
-            pltpu.VMEM(product.shape, BF16), pltpu.VMEM((tall, length), F32), pltpu.VMEM((tall, length), BF16),
+            pltpu.VMEM((near, own * per, length), BF16), pltpu.VMEM((near, own * per, length), BF16),
+            pltpu.VMEM((tall, length), F32), pltpu.VMEM((tall, length), BF16),
             pltpu.VMEM((length, channels), jnp.int32),
+            pltpu.VMEM((nq, nr, tall, length), BF16), pltpu.VMEM((HEADS, length, length), F32),
+            rows_bf16, rows_bf16, rows_bf16, rows_bf16, rows_bf16, rows_bf16,
             dma((chunks, near - 1)), dma((chunks, near - 1)), dma((chunks,)),
             dma((max(nr - 1, 1),)), dma((max(nr - 1, 1),)),
             dma((max(nc - 1, 1),)), dma((max(nc - 1, 1),)),
             dma((nc, max(ns - 1, 1))), dma((nc, max(ns - 1, 1))), dma,
-        ],
+            dma((chunks, nq - 1)), dma((chunks, nq - 1)), dma((chunks,)),
+        ]
+        + [pltpu.VMEM((tall_left, 128), F32)] * lanes
+        + [pltpu.VMEM((tall_right, 128), F32)] * lanes
+        + [pltpu.VMEM((tall_left, 128), F32)] * lanes,
         compiler_params=params(2),
-        name="update",
-    )(chain_ids, pair_rows, product, chain_row, live_row, chain_one, tri_gate, tri_out, bias_weight)
-    bias_all = jnp.transpose(bias_all.reshape(nq, nr, HEADS, own, length), (2, 1, 0, 3, 4))
-    bias_all = bias_all.reshape(HEADS, length, length).astype(F32)
-    return pl.pallas_call(
-        functools.partial(attend_kernel, sizes),
-        in_specs=[vmem] * 6,
-        out_specs=anywhere,
-        out_shape=jax.ShapeDtypeStruct((rows, cols, channels), BF16),
-        scratch_shapes=[
-            pltpu.VMEM(row_shape.shape, BF16),
-            dma((chunks, nq - 1)), dma((chunks, nq - 1)), dma((chunks,)),
-        ],
-        compiler_params=params(3),
-        name="attend",
-    )(second, after, bias_all, att_query, att_kv, att_out)
+        name="finish",
+    )(
+        chain_ids, left.reshape(tall_left, length), right.reshape(tall_right, length), pair_rows,
+        chain_row, live_row, chain_one, tri_gate, tri_out, bias_weight, att_query, att_kv, att_out,
+    )
 
 
 def device_program(sizes, pair, *rest):

time: 253 us -> 238 us (0.941)
  Pallas kernels: 241 us -> 228 us
    pallas_call x3 -> x1, Pallas kernels: 115 us -> 102 us  [by_rows(): pl.pallas_call(functools.partial(finish_kernel, sizes), in_specs=[smem] +...]
    convert_element_type x1 -> x0, local copies, waits for them, and re-layouts: 2.93 us -> none  [by_rows(): bias_all = bias_all.reshape(HEADS, length, length).astype(F32)]
where the time goes in v4:
time: 238 us; the launch traced here: 237 us
  Pallas kernels  228 us (96%)
  local copies, waits for them, and re-layouts  8.16 us (3%)
    pallas_call x1, Pallas kernels, by_rows(): pl.pallas_call(functools.partial(project_kernel, sizes), in_specs=[smem,...  125 us
    pallas_call x1, Pallas kernels, by_rows(): pl.pallas_call(functools.partial(finish_kernel, sizes), in_specs=[smem] +...  102 us

profile of v4, /device:TPU:25, one launch (start us, length us, event | category | flops | bytes accessed | tf_op | source)
XLA Modules:
  0.0 236.6 jit_solution(7123457581905125104)
XLA Ops:
  0.0 1.2 broadcast_in_dim.10.live_row
  1.2 1.2 broadcast_in_dim.9.chain_row
  2.4 1.2 pad.4.att_bias
  3.7 0.8 fusion
  4.5 0.1 copy.16
  4.6 0.1 copy.18
  4.7 0.1 copy.17
  4.8 0.1 copy.19
  5.0 0.7 maximum_bitcast_fusion.weight
  5.6 125.3 %project.1 = (bf16[24,384,128]{2,1,0:T(8,128)(2,1)}, bf16[8,24,16,384]{3,2,1,0:T(8,128)(2,1)}, bf16[16,24,16,384]{3,2,1,0:T(8,128)(2,1)}) custom-call(s32[384]{0:T(512)} %chain_ids.3, s32[384]{0:T(512)} %residue_mask.1, s32[1,384]{1,0:T(1,128)} %broadcast_in_dim.9.chain_row, s32[1,384]{1,0:T(1,128)} %broadcast_in_dim.10.live_row, f32[1,128]{1,0:T(1,128)} %bitcast.8, ...), custom_call_target="tpu_custom_call" | custom-call | tf_op jit(solution)/shard_map/project/pallas_call | solution.py:514
  131.0 102.4 %finish.1 = bf16[96,96,128]{2,1,0:T(8,128)(2,1)} custom-call(s32[384]{0:T(512)} %chain_ids.3, bf16[3072,384]{1,0:T(8,128)(2,1)} %bitcast.7, bf16[6144,384]{1,0:T(8,128)(2,1)} %bitcast.6, bf16[24,384,128]{2,1,0:T(8,128)(2,1)} %get-tuple-element.10.pair_ref, s32[1,384]{1,0:T(1,128)} %broadcast_in_dim.9.chain_row, s32[1,384]{1,0:T(1,128)} %broadcast_in_dim.10.live_row, ...), custom_call_target="tpu_custom_call" | custom-call | tf_op jit(solution)/shard_map/finish/pallas_call | solution.py:536
  233.4 3.2 %copy.21 = bf16[96,96,128]{2,1,0:T(8,128)(2,1)} copy(bf16[96,96,128]{2,1,0:T(8,128)(2,1)} %finish.1) | data formatting | bytes 4718592

commit v5 on v4

--- a/solution.py
+++ b/solution.py
@@ -187,7 +187,7 @@
 
 
 def columns_of(ids):
-    spread = jnp.broadcast_to(ids.astype(F32), (128, ids.shape[1]))
+    spread = jnp.broadcast_to(ids.astype(F32)[None, :], (128, ids.shape[0]))
     return spread.T.astype(jnp.int32)
 
 
@@ -241,7 +241,7 @@
         mine.start()
         arriving.append((now, mine))
     chain_cols[...] = columns_of(chain_row[...])
-    live_cols = live_row[...].astype(F32)
+    live_cols = live_row[...].astype(F32)[None, :]
     leaving = []
     for n in range(chunks):
         now, mine = arriving[n]
@@ -353,7 +353,7 @@
         mine.start()
         arriving.append((now, mine))
     chain_cols[...] = columns_of(chain_row[...])
-    live_cols = live_row[...].astype(F32)
+    live_cols = live_row[...].astype(F32)[None, :]
     for n in range(chunks):
         now, mine = arriving[n]
         mine.wait()
@@ -376,7 +376,7 @@
             second = norm_rows(after.astype(F32)).astype(BF16)
             after_ref[i] = after
             second_ref[i] = second
-            bias = dot(att_bias[...], second, NT)
+            bias = dot(att_bias[...], second, (((0,), (1,)), ((), ())))
             bias = jnp.where(live_cols > 0.0, bias, MASKED)
             for h in range(HEADS):
                 bias_ref[pl.ds(h * own + i, 1), :] = bias[h : h + 1, :]
@@ -495,10 +495,9 @@
     length = cols * nq
     near = groups // 2
     per = channels // near
-    chain_row, live_row, chain_one = chain_ids[None, :], residue_mask[None, :], chain_vec[None, :]
+    chain_row, live_row, chain_one = chain_ids, residue_mask, chain_vec[None, :]
     order = [tri_in[:, n * channels : (n + 1) * channels] for n in (0, 2, 1, 3)]
     weight = jnp.concatenate(order, axis=1).T
-    bias_weight = jnp.pad(att_bias.T, ((0, 8 - HEADS), (0, 0)))
 
     chunks = own // CHUNK
     smem = pl.BlockSpec(memory_space=pltpu.SMEM)
@@ -557,7 +556,7 @@
         name="finish",
     )(
         chain_ids, left.reshape(tall_left, length), right.reshape(tall_right, length), pair_rows,
-        chain_row, live_row, chain_one, tri_gate, tri_out, bias_weight, att_query, att_kv, att_out,
+        chain_row, live_row, chain_one, tri_gate, tri_out, att_bias, att_query, att_kv, att_out,
     )
 
 

time: 238 us -> 236 us (level)
    broadcast_in_dim x2 -> x0, local copies, waits for them, and re-layouts: 2.43 us -> none  [the longest x1 1.22 us: by_rows(): chain_ids[None, :]]
    unnamed x5 -> x6, local copies, waits for them, and re-layouts: 3.69 us -> 5.08 us
where the time goes in v5:
time: 236 us; the launch traced here: 235 us
  Pallas kernels  229 us (97%)
  local copies, waits for them, and re-layouts  5.9 us (2%)
    pallas_call x1, Pallas kernels, by_rows(): pl.pallas_call(functools.partial(project_kernel, sizes), in_specs=[smem,...  125 us
    pallas_call x1, Pallas kernels, by_rows(): pl.pallas_call(functools.partial(finish_kernel, sizes), in_specs=[smem] +...  103 us
    unnamed x6, local copies, waits for them, and re-layouts  5.08 us

profile of v5, /device:TPU:25, one launch (start us, length us, event | category | flops | bytes accessed | tf_op | source)
XLA Modules:
  0.0 235.2 jit_solution(2690139443020001312)
XLA Ops:
  0.0 1.4 copy.16.att_bias
  1.4 0.8 fusion
  2.2 0.1 copy.17
  2.3 0.1 copy.19
  2.5 0.1 copy.18
  2.6 0.1 copy.20
  2.7 0.7 maximum_bitcast_fusion.weight
  3.4 125.5 %project.1 = (bf16[24,384,128]{2,1,0:T(8,128)(2,1)}, bf16[8,24,16,384]{3,2,1,0:T(8,128)(2,1)}, bf16[16,24,16,384]{3,2,1,0:T(8,128)(2,1)}) custom-call(s32[384]{0:T(512)} %chain_row.3, s32[384]{0:T(512)} %live_row.3, s32[384]{0:T(512)} %chain_row.3, s32[384]{0:T(512)} %live_row.3, f32[1,128]{1,0:T(1,128)} %bitcast.7, ...), custom_call_target="tpu_custom_call" | custom-call | tf_op jit(solution)/shard_map/project/pallas_call | solution.py:513
  128.9 103.1 %finish.1 = bf16[96,96,128]{2,1,0:T(8,128)(2,1)} custom-call(s32[384]{0:T(512)} %chain_row.3, bf16[3072,384]{1,0:T(8,128)(2,1)} %bitcast.6, bf16[6144,384]{1,0:T(8,128)(2,1)} %bitcast.5, bf16[24,384,128]{2,1,0:T(8,128)(2,1)} %get-tuple-element.10.pair_ref, s32[384]{0:T(512)} %chain_row.3, s32[384]{0:T(512)} %live_row.3, f32[1,128]{1,0:T(1,128)} %bitcast.8, ...), custom_call_target="tpu_custom_call" | custom-call | tf_op jit(solution)/shard_map/finish/pallas_call | solution.py:535
  232.0 3.2 %copy.22 = bf16[96,96,128]{2,1,0:T(8,128)(2,1)} copy(bf16[96,96,128]{2,1,0:T(8,128)(2,1)} %finish.1) | data formatting | bytes 4718592
